TPU v7x, 128 devices: a whole 4x4x4 slice. The times are simulated.
128 devices in a mesh: row: 8 (over x_hi, y), col: 16 (over z, x_lo, core).
Axes of the slice: x: 4 (x_hi: 2, x_lo: 2; x = x_hi * 2 + x_lo), y: 4, z: 4, core: 2. Of those that a mesh axis runs over, the one named last changes fastest.
Arguments:
- tokens: bfloat16 [16384, 2880], P(('col', 'row')), may hold values from -6 to 6
- seg_ids: int32 [16384], P(('col', 'row')), may hold values from 0 to 15, never falling along the last dimension, each value on 1 to 2048 neighbouring positions
- norm_gain: float32 [2880], replicated, may hold values from 0.1 to 1.9
- query_weight: bfloat16 [2880, 4096], P('col', 'row'), may hold values from -4.5839394 to 4.5839394
- kv_weight: bfloat16 [2880, 1024], P('col', 'row'), may hold values from -0.1118034 to 0.1118034
- out_weight: bfloat16 [4096, 2880], P('row', 'col'), may hold values from -0.09375 to 0.09375
- sinks: float32 [64], P('row'), may hold values from 1 to 6
- moe_gain: float32 [2880], replicated, may hold values from 0.1 to 1.9
- routes: int32 [16384, 4], P(('col', 'row')), may hold values from 0 to 63, all different within a row; in each aligned block of 128 rows (0 to 127, 128 to 255, ...) at most 9 rows name the same one
- route_weights: float32 [16384, 4], P(('col', 'row')), may hold values from 0.05 to 0.5
- expert_in: bfloat16 [128, 2880, 1536], P(('row', 'col')), may hold values from -0.109375 to 0.109375
- expert_out: bfloat16 [128, 768, 2880], P(('row', 'col')), may hold values from -0.21875 to 0.21875
Outputs:
- mixed: bfloat16 [16384, 2880], P(('col', 'row'))
- kv_cache: bfloat16 [16384, 1024], P('col', 'row')
Inputs may be any that keep to these rules, and one draw needn't show every extreme that they name: `seg_ids`: never falling; each prompt has 1 to 2048 tokens, one exactly 2048. `routes`: each row names 4 different experts; among the 128 rows of one device no expert is named more than 9 times, and on some device one is named exactly 9 times.
All inputs are finite; a program needn't handle non-finite values.
Results may differ from a plain program's by a relative error of at most 0.012.
Values may be sent and summed in bfloat16 or wider, within the bound.
A program may use at most 128 MiB of HBM per device.

v0:
```python
import math

import jax
import jax.numpy as jnp
from jax import lax
from jax.sharding import PartitionSpec as P

HD = 64
WIN = 128
EXPERTS = 64
TOP = 4
CAP = 9


eps_norm = 1e-05
theta_base = 150000.0
glu_alpha = 1.702
masked_score = -1e30


def entering(part, axis, combine, identity):
    place = lax.axis_index(axis)
    gathered = jax.tree.map(lambda a: lax.all_gather(a, axis), part)
    state = jax.tree.map(lambda a, e: jnp.zeros_like(a) + jnp.asarray(e, a.dtype), part, identity)

    def one(step, state):
        return combine(
            state, jax.tree.map(lambda a: lax.dynamic_index_in_dim(a, step, 0, False), gathered)
        )

    return lax.fori_loop(0, place, one, state)


def from_behind(value, axis, steps):
    count = lax.axis_size(axis)
    first, last = (max(0, -steps), min(count, count - steps))
    return lax.ppermute(value, axis, [(source, source + steps) for source in range(first, last)])


def rms_scale(values_in, gain_vec):
    widened = values_in.astype(jnp.float32)
    return (
        widened
        * lax.rsqrt(jnp.mean(widened * widened, axis=-1, keepdims=True) + eps_norm)
        * gain_vec
    )


def rotate(values_in, positions):
    half_dim = values_in.shape[-1] // 2
    frequency = jnp.exp(
        jnp.arange(half_dim, dtype=jnp.float32)
        * (-2.0 * math.log(theta_base) / values_in.shape[-1])
    )
    angles = positions.astype(jnp.float32)[:, None] * frequency[None, :]
    cosine = jnp.cos(angles)[:, None, :]
    sine = jnp.sin(angles)[:, None, :]
    first_half = values_in[..., :half_dim]
    second_half = values_in[..., half_dim:]
    return jnp.concatenate(
        [first_half * cosine - second_half * sine, second_half * cosine + first_half * sine],
        axis=-1,
    )


def joined(earlier, later):
    first_early, last_early, start_early = earlier
    first_late, last_late, start_late = later
    first_seg = jnp.where(first_early < 0, first_late, first_early)
    last_seg = jnp.where(last_late < 0, last_early, last_late)
    carried = (first_late == last_late) & (last_early == first_late) | (first_late < 0)
    return (first_seg, last_seg, jnp.where(carried, start_early, start_late))


def attend_tile(
    query_tile, key_tile, value_tile, query_seg, key_seg, query_pos, key_pos, sink_grid
):
    scores = jnp.einsum(
        "qkgd,lkd->kgql", query_tile, key_tile, preferred_element_type=jnp.float32
    ) * query_tile.shape[-1] ** (-0.5)
    distance = query_pos[:, None] - key_pos[None, :]
    allowed = (
        (query_seg[:, None] == key_seg[None, :])
        & (distance >= 0)
        & (distance < WIN)
        & (key_pos[None, :] >= 0)
    )
    scores = jnp.where(allowed[None, None], scores, masked_score)
    sink_col = sink_grid[:, :, None]
    ceiling = jnp.maximum(jnp.max(scores, axis=-1), sink_col)
    expo = jnp.exp(scores - ceiling[..., None])
    denom = jnp.sum(expo, axis=-1) + jnp.exp(sink_col - ceiling)
    probs = (expo / denom[..., None]).astype(jnp.bfloat16)
    return jnp.einsum(
        "kgql,lkd->qkgd", probs, value_tile, preferred_element_type=jnp.float32
    ).astype(jnp.bfloat16)


def expert_block(arrived, expert_in, expert_out):
    half_width = expert_out.shape[1]
    mixed_in = jnp.einsum("nscd,sdf->nscf", arrived, expert_in, preferred_element_type=jnp.float32)
    gate_part = mixed_in[..., :half_width]
    up_part = mixed_in[..., half_width:]
    hidden_act = (gate_part * jax.nn.sigmoid(glu_alpha * gate_part) * (up_part + 1.0)).astype(
        jnp.bfloat16
    )
    return jnp.einsum(
        "nscf,sfd->nscd", hidden_act, expert_out, preferred_element_type=jnp.float32
    ).astype(jnp.bfloat16)


def shards(
    tokens,
    seg_ids,
    norm_gain,
    query_weight,
    kv_weight,
    out_weight,
    sinks,
    moe_gain,
    routes,
    route_weights,
    expert_in,
    expert_out,
):
    feature_dim = tokens.shape[1]
    normed = rms_scale(tokens, norm_gain).astype(jnp.bfloat16)
    block_x, block_seg = (
        lax.all_gather(normed, "row", axis=0, tiled=True),
        lax.all_gather(seg_ids, "row", axis=0, tiled=True),
    )
    block_rows = block_x.shape[0]
    base_index = lax.axis_index("col") * block_rows
    token_index = base_index + jnp.arange(block_rows, dtype=jnp.int32)
    before = jnp.concatenate([block_seg[:1], block_seg[:-1]])
    own_start = lax.cummax(jnp.where(block_seg != before, token_index, base_index))
    summary = (block_seg[0], block_seg[block_rows - 1], own_start[block_rows - 1])
    neutral = (jnp.int32(-1), jnp.int32(-1), jnp.int32(-1))
    prior = entering(summary, "col", joined, neutral)
    lead_start = jnp.where(prior[1] == block_seg[0], prior[2], base_index)
    positions = token_index - jnp.where(own_start == base_index, lead_start, own_start)
    query_cols = query_weight.shape[1]
    kv_cols = kv_weight.shape[1]
    query_sum = jnp.dot(
        block_x,
        lax.all_gather(query_weight, "col", axis=0, tiled=True),
        preferred_element_type=jnp.float32,
    )
    kv_sum = jnp.dot(
        block_x,
        lax.all_gather(kv_weight, "col", axis=0, tiled=True),
        preferred_element_type=jnp.float32,
    )
    query_heads = query_cols // HD
    kv_heads = kv_cols // (2 * HD)
    group_size = query_heads // kv_heads
    queries = rotate(query_sum.reshape(block_rows, query_heads, HD), positions).astype(jnp.bfloat16)
    kv_pair = kv_sum.reshape(block_rows, kv_heads, 2, HD)
    keys = rotate(kv_pair[:, :, 0], positions).astype(jnp.bfloat16)
    values = kv_pair[:, :, 1].astype(jnp.bfloat16)
    kv_cache = jnp.stack([keys, values], axis=2).reshape(block_rows, kv_cols)
    edge_kv, edge_seg = from_behind(
        (kv_cache[block_rows - WIN :], block_seg[block_rows - WIN :]), "col", 1
    )
    all_kv = jnp.concatenate([edge_kv, kv_cache], axis=0).reshape(WIN + block_rows, kv_heads, 2, HD)
    all_seg = jnp.concatenate([edge_seg, block_seg])
    key_index = base_index - WIN + jnp.arange(WIN + block_rows, dtype=jnp.int32)
    span_rows = math.gcd(block_rows, 512)
    query_grid = queries.reshape(block_rows // span_rows, span_rows, kv_heads, group_size, HD)
    sink_grid = sinks.reshape(kv_heads, group_size)

    def attend_step(step_id):
        first_row = step_id * span_rows
        query_tile = lax.dynamic_index_in_dim(query_grid, step_id, 0, keepdims=False)
        kv_tile = lax.dynamic_slice_in_dim(all_kv, first_row, span_rows + WIN, 0)
        key_seg = lax.dynamic_slice_in_dim(all_seg, first_row, span_rows + WIN, 0)
        key_pos = lax.dynamic_slice_in_dim(key_index, first_row, span_rows + WIN, 0)
        query_seg = lax.dynamic_slice_in_dim(block_seg, first_row, span_rows, 0)
        query_pos = lax.dynamic_slice_in_dim(token_index, first_row, span_rows, 0)
        tile_out = attend_tile(
            query_tile,
            kv_tile[:, :, 0],
            kv_tile[:, :, 1],
            query_seg,
            key_seg,
            query_pos,
            key_pos,
            sink_grid,
        )
        return tile_out.reshape(span_rows, query_cols)

    attended = lax.map(attend_step, jnp.arange(block_rows // span_rows, dtype=jnp.int32)).reshape(
        block_rows, query_cols
    )
    partial_value = jnp.dot(
        attended,
        lax.all_gather(out_weight, "col", axis=1, tiled=True),
        preferred_element_type=jnp.float32,
    )
    head_total = lax.psum_scatter(
        partial_value.astype(jnp.bfloat16), "row", scatter_dimension=0, tiled=True
    ).astype(jnp.float32)
    hidden = tokens.astype(jnp.float32) + head_total
    moe_in = rms_scale(hidden, moe_gain).astype(jnp.bfloat16)
    route_flat = routes.reshape(-1)
    route_count = route_flat.shape[0]
    expert_ids = jnp.arange(EXPERTS, dtype=jnp.int32)
    hit_table = (route_flat[:, None] == expert_ids[None, :]).astype(jnp.int32)
    slot_ranks = jnp.sum((jnp.cumsum(hit_table, axis=0) - hit_table) * hit_table, axis=1)
    slot_index = route_flat * CAP + slot_ranks
    slot_table = (
        jnp.full((EXPERTS * CAP,), route_count, jnp.int32)
        .at[slot_index]
        .set(jnp.arange(route_count, dtype=jnp.int32))
    )
    padded_rows = jnp.concatenate([moe_in, jnp.zeros((1, feature_dim), jnp.bfloat16)], axis=0)
    outgoing = padded_rows[slot_table // TOP]
    outgoing = jnp.broadcast_to(
        outgoing.reshape(EXPERTS, 1, CAP, feature_dim), (EXPERTS, 2, CAP, feature_dim)
    )
    slices_here = expert_in.shape[0]
    row_count = lax.axis_size("row")
    col_count = lax.axis_size("col")
    device_count = row_count * col_count
    outgoing = outgoing.reshape(device_count, slices_here, CAP, feature_dim)
    arrived = lax.all_to_all(outgoing, ("row", "col"), split_axis=0, concat_axis=0, tiled=True)
    produced = expert_block(arrived, expert_in, expert_out)
    returned = lax.all_to_all(produced, ("row", "col"), split_axis=0, concat_axis=0, tiled=True)
    combined = jnp.sum(
        returned.reshape(EXPERTS, 2, CAP, feature_dim).astype(jnp.float32), axis=1
    ).reshape(EXPERTS * CAP, feature_dim)
    weighted = combined[slot_index] * route_weights.reshape(-1)[:, None]
    expert_total = jnp.sum(weighted.reshape(-1, TOP, feature_dim), axis=1)
    mixed = (hidden + expert_total).astype(jnp.bfloat16)
    return (mixed, kv_cache)


def solution(mesh):
    in_specs = (
        P(("col", "row"), None),
        P(("col", "row")),
        P(),
        P("col", "row"),
        P("col", "row"),
        P("row", "col"),
        P("row"),
        P(),
        P(("col", "row"), None),
        P(("col", "row"), None),
        P(("row", "col"), None, None),
        P(("row", "col"), None, None),
    )
    out_specs = (P(("col", "row"), None), P("col", "row"))
    return jax.shard_map(shards, mesh=mesh, in_specs=in_specs, out_specs=out_specs, check_vma=False)
```

profile of v0, /device:TPU:51, one launch (start us, length us, event | category | flops | bytes accessed | tf_op | source)
XLA Modules:
  0.0 854.7 jit_solution(16961109207965184848)
XLA Ops:
  8.7 1.5 copy.51
  10.4 1.9 fusion.33
  12.3 14.9 %all-gather.1 = s32[8,1,128]{2,1,0:T(1,128)S(1)} all-gather(s32[1,1,128]{2,1,0:T(1,128)} %bitcast.185), channel_id=1, replica_groups=mesh['row'=8,'col'=16] {'row'}, dimensions={0}, use_global_device_ids=true | all-gather | bytes 4608 | tf_op jit(solution)/shard_map/all_gather | solution.py:130
  27.3 8.1 collective-permute-start.1
  40.8 8.1 all-reduce.4
  48.9 41.8 %while.24 = (s32[]{:T(128)}, s32[]{:T(128)}, s32[]{:T(128)}, s32[]{:T(128)}, s32[16]{0:T(128)S(1)}, /*index=5*/s32[16]{0:T(128)S(1)}, s32[16]{0:T(128)S(1)}, s32[]{:T(128)}, s32[]{:T(128)}, s32[]{:T(128)}) while((s32[]{:T(128)}, s32[]{:T(128)}, s32[]{:T(128)}, s32[]{:T(128)}, s32[16]{0:T(128)S(1)}, /*index=5*/s32[16]{0:T(128)S(1)}, ...), condition=%wide.region_4.5_spmd, body=%wide.region_3.4_spmd.sunk | while | flops 13 | bytes 239 | solution.py:31
  92.0 68.1 %all-gather = bf16[16,180,128]{2,1,0:T(8,128)(2,1)S(1)} all-gather(bf16[1,180,128]{2,1,0:T(8,128)(2,1)S(1)} %bitcast.179), channel_id=1, replica_groups=mesh['row'=8,'col'=16] {'col'}, dimensions={0}, use_global_device_ids=true | all-gather | bytes 783360 | tf_op jit(solution)/shard_map/all_gather | solution.py:151
  160.8 4.4 reshape.540
  165.2 4.3 reshape.542
  169.5 3.1 all-gather.8.cloned.1.call-done
  172.6 5.0 fusion.56
  177.9 3.4 fusion.57
  183.1 7.4 collective-permute-start
  190.5 1.4 pad_maximum_fusion
  192.1 39.1 %while.25 = (s32[]{:T(128)}, bf16[2,512,512]{2,1,0:T(8,128)(2,1)}, s32[2]{0:T(128)S(1)}, bf16[1152,1,2,64]{0,3,2,1:T(8,128)(2,1)S(1)}, s32[1024]{0:T(1024)}, /*i...) while((s32[]{:T(128)}, bf16[2,512,512]{2,1,0:T(8,128)(2,1)}, ...), condition=%wide.region_8.9_spmd, body=%wide.region_5.8_spmd.sunk | while | flops 705110656 | bytes 78284200 | solution.py:192
  197.7 1.8 fusion.71
  199.6 2.2 fusion.72
  201.8 1.7 copy-done
  203.6 7.0 fusion.73
  217.2 1.7 fusion.71
  219.0 2.2 fusion.72
  221.2 1.7 copy-done
  223.0 7.1 fusion.73
  231.2 8.0 convolution_convert_fusion
  239.2 8.5 copy.71
  250.6 2.7 scatter_custom_fusion
  253.3 88.8 %reduce-scatter.4.cloned.1.call-done = bf16[128,2880]{1,0:T(8,128)(2,1)} async-done(((bf16[1024,2880]{1,0:T(8,128)(2,1)}), bf16[128,2880]{1,0:T(8,128)(2,1)}) %reduce-scatter.4.cloned.1.call-update) | async-done | bytes 737296 | tf_op jit(solution)/shard_map/reduce_scatter | solution.py:200
  342.0 1.4 multiply_reduce_fusion.1
  343.5 1.4 multiply_convert_fusion
  345.0 4.5 gather_fusion
  349.5 7.2 broadcast_in_dim.44
  356.6 4.5 broadcast_in_dim.45.clone
  361.1 145.1 %all_to_all.10 = bf16[128,1,9,2880]{3,2,1,0:T(8,128)(2,1)} all-to-all(bf16[128,1,9,2880]{3,2,1,0:T(8,128)(2,1)S(1)} %bitcast.165), channel_id=1, replica_groups=mesh['row'=8,'col'=16] {'row','col'}, dimensions={0} | all-to-all | bytes 13271040 | tf_op jit(solution)/shard_map/all_to_all | solution.py:226
  506.3 15.7 %copy.61 = bf16[128,1,9,2880]{0,3,2,1:T(8,128)(2,1)} copy(bf16[128,1,9,2880]{3,2,1,0:T(8,128)(2,1)} %all_to_all.10) | data formatting | bytes 13271040 | tf_op jit(solution)/shard_map/all_to_all | solution.py:226
  522.0 16.5 %fusion.20 = f32[128,1,9,1536]{3,0,2,1:T(8,128)S(1)} fusion(bf16[1,2880,1536]{2,1,0:T(8,128)(2,1)} %param.26, bf16[128,1,9,2880]{0,3,2,1:T(8,128)(2,1)} %copy.61), kind=kOutput, calls=%fused_computation.35 | convolution fusion | flops 10192158720 | bytes 22560768 | tf_op jit(solution)/shard_map/nscd,sdf->nscf/dot_general | solution.py:101
  538.5 8.2 convert_bitcast_fusion
  546.8 15.1 %copy.62 = bf16[128,1,9,2880]{3,2,1,0:T(8,128)(2,1)} copy(bf16[128,1,9,2880]{0,3,2,1:T(8,128)(2,1)} %convert_bitcast_fusion) | data formatting | bytes 13271040 | tf_op jit(solution)/shard_map/convert_element_type | solution.py:109
  561.8 13.4 %all-to-all-start.1 = ((bf16[128,1,9,2880]{3,2,1,0:T(8,128)(2,1)}), bf16[128,1,9,2880]{3,2,1,0:T(8,128)(2,1)}, u32[]{:S(2)}, u32[]{:S(2)}) async-start(bf16[128,1,9,2880]{3,2,1,0:T(8,128)(2,1)} %copy.62), calls=%async_computation.1 | async-start | bytes 24117248 | tf_op jit(solution)/shard_map/all_to_all | solution.py:228
  576.2 160.5 %all-to-all-done.1 = bf16[128,1,9,2880]{3,2,1,0:T(8,128)(2,1)} async-done(((bf16[128,1,9,2880]{3,2,1,0:T(8,128)(2,1)}), bf16[128,1,9,2880]{3,2,1,0:T(8,128)(2,1)}, u32[]{:S(2)}, u32[]{:S(2)}) %all-to-all-start.1) | async-done | bytes 6635552 | tf_op jit(solution)/shard_map/all_to_all | solution.py:228
  736.7 15.7 %copy.63 = bf16[128,1,9,2880]{0,3,2,1:T(8,128)(2,1)} copy(bf16[128,1,9,2880]{3,2,1,0:T(8,128)(2,1)} %all-to-all-done.1) | data formatting | bytes 13271040 | tf_op jit(solution)/shard_map/all_to_all | solution.py:228
  752.5 10.4 %copy.64 = f32[128,1,9,2880]{3,0,2,1:T(8,128)} copy(bf16[128,1,9,2880]{0,3,2,1:T(8,128)(2,1)} %copy.63) | data formatting | bytes 19906560 | tf_op jit(solution)/shard_map/convert_element_type | solution.py:230
  762.9 16.0 %reshape.500 = f32[64,2,9,2880]{3,1,0,2:T(2,128)} reshape(f32[128,1,9,2880]{3,0,2,1:T(8,128)} %copy.64) | data formatting | bytes 26542080 | tf_op jit(solution)/shard_map/convert_element_type | solution.py:230
  778.9 21.8 %reduce_sum.60 = f32[64,9,2880]{2,0,1:T(8,128)} reduce(f32[64,2,9,2880]{3,1,0,2:T(2,128)} %reshape.500, f32[]{:T(128)} %constant.90.clone.1), dimensions={1}, to_apply=%region_15.16 | reduce | flops 1658880 | bytes 19906564 | tf_op jit(solution)/shard_map/reduce_sum | solution.py:229
  800.7 11.6 %copy.65 = f32[64,9,2880]{2,1,0:T(8,128)} copy(f32[64,9,2880]{2,0,1:T(8,128)} %reduce_sum.60) | data formatting | bytes 13271040 | tf_op jit(solution)/shard_map/reduce_sum | solution.py:229
  812.3 9.5 %reshape.498 = f32[576,2880]{1,0:T(8,128)} reshape(f32[64,9,2880]{2,1,0:T(8,128)} %copy.65) | data formatting | bytes 13271040 | tf_op jit(solution)/shard_map/reshape | solution.py:231
  821.8 9.9 %gather_fusion.1 = f32[512,2880]{1,0:T(8,128)} fusion(f32[576,2880]{1,0:T(8,128)} %reshape.498, s32[1024]{0:T(1024)S(1)} %pad_clamp_fusion), kind=kCustom, calls=%fused_computation.1 | custom fusion | bytes 11798528 | tf_op jit(solution)/shard_map/gather | solution.py:232
  831.7 7.8 gather.10
  839.5 7.2 multiply_reduce_fusion
  (158 shorter events, 36.7 us)
Async XLA Ops:
  7.2 84.8 %copy-start.12 = (bf16[180,128]{1,0:T(8,128)(2,1)S(1)}, bf16[180,128]{1,0:T(8,128)(2,1)}, u32[]{:S(2)}) copy-start(bf16[180,128]{1,0:T(8,128)(2,1)} %param.20) | copy-start | bytes 138244
  7.2 153.6 %all-gather.10.cloned.1.call-start = ((), (), s32[]{:S(2)}) async-start(), calls=%async_computation.4 | async-start | bytes 3203072 | tf_op jit(solution)/shard_map/all_gather | solution.py:146
  7.9 157.3 %all-gather.12.cloned.1.call-start = ((), (), s32[]{:S(2)}) async-start(), calls=%async_computation.5 | async-start | bytes 3203072 | tf_op jit(solution)/shard_map/all_gather | solution.py:197
  8.7 163.9 %all-gather.8.cloned.1.call-start = ((), (), s32[]{:S(2)}) async-start(), calls=%async_computation.3 | async-start | bytes 6782976 | tf_op jit(solution)/shard_map/all_gather | solution.py:129
  12.3 329.7 %reduce-scatter.4.cloned.1.call-start = ((), (), s32[]{:S(2)}) async-start(), calls=%async_computation.6 | async-start | bytes 6782976 | tf_op jit(solution)/shard_map/reduce_scatter | solution.py:200
  27.3 142.2 %copy-start.6 = (s32[8,1,128]{2,1,0:T(1,128)}, s32[8,1,128]{2,1,0:T(1,128)S(1)}, u32[]{:S(2)}) copy-start(s32[8,1,128]{2,1,0:T(1,128)S(1)} %all-gather.1) | copy-start | bytes 12292
  27.3 132.9 %collective-permute-start.1 = (s32[128]{0:T(128)S(1)}, s32[128]{0:T(128)S(1)}, u32[]{:S(2)}, u32[]{:S(2)}) collective-permute-start(s32[128]{0:T(128)S(1)} %slice_bitcast_fusion.1), channel_id=1, source_target_pairs={{0,1},{1,2},{2,3},{3,4},{4,5},{5,6},{6,7},{7,8},{8,9},{9,10},{10,1... | collective-permute-start | bytes 1544 | tf_op jit(solution)/shard_map/ppermute | solution.py:37
  172.6 5.0 copy-start.1
  172.6 5.3 copy-start.3
  183.0 9.0 %copy-start.4 = (bf16[1024,1,2,64]{0,3,2,1:T(8,128)(2,1)}, bf16[1024,1,2,64]{0,3,2,1:T(8,128)(2,1)S(1)}, u32[]{:S(2)}) copy-start(bf16[1024,1,2,64]{0,3,2,1:T(8,128)(2,1)S(1)} %pad_maximum_fusion.1) | copy-start | bytes 786436
  183.1 9.0 %collective-permute-start = (bf16[128,128]{0,1:T(8,128)(2,1)S(1)}, bf16[128,128]{0,1:T(8,128)(2,1)S(1)}, u32[]{:S(2)}, u32[]{:S(2)}) collective-permute-start(bf16[128,128]{0,1:T(8,128)(2,1)S(1)} %bitcast.181), channel_id=1, source_target_pairs={{0,1},{1,2},{2,3},{3,4},{4,5},{5,6},{6,7},{7,8},{8,9},{9,10},{10,1... | collective-permute-start | bytes 98312 | tf_op jit(solution)/shard_map/ppermute | solution.py:37
  192.3 1.3 copy-start.7
  192.3 2.2 copy-start.10
  197.7 1.8 copy-start.9
  199.5 4.0 copy-start
  203.6 8.1 copy-start.8
  203.6 8.1 copy-start.11
  211.7 1.3 copy-start.7
  211.7 2.2 copy-start.10
  217.2 1.8 copy-start.9
  218.9 4.0 copy-start
  223.0 8.2 copy-start.8
  223.0 8.2 copy-start.11
  247.7 0.7 copy-start.14
  247.7 95.8 %copy-start.13 = (f32[2880]{0:T(1024)S(1)}, f32[2880]{0:T(1024)}, u32[]{:S(2)}) copy-start(f32[2880]{0:T(1024)} %param.23) | copy-start | bytes 34564
  506.3 32.2 %slice-start = ((s8[4423680]{0:T(1024)(128)(4,1)}), s8[229376]{0:T(1024)(128)(4,1)S(1)}, s32[]{:S(2)}) async-start(s8[4423680]{0:T(1024)(128)(4,1)} %bitcast.186), calls=%async_computation.7 | async-start | bytes 458752
  522.0 16.6 %slice-start.1 = ((s8[4423680]{0:T(1024)(128)(4,1)}), s8[4194304]{0:T(1024)(128)(4,1)S(1)}, s32[]{:S(2)}) async-start(s8[4423680]{0:T(1024)(128)(4,1)} %bitcast.186), calls=%async_computation.8 | async-start | bytes 8388608
  561.8 13.4 %copy-start.15 = (f32[128,4]{0,1:T(4,128)S(1)}, f32[128,4]{0,1:T(4,128)}, u32[]{:S(2)}) copy-start(f32[128,4]{0,1:T(4,128)} %param.25) | copy-start | bytes 6148
  561.8 13.5 %copy-start.5 = (bf16[1024,1,2,64]{0,3,2,1:T(8,128)(2,1)S(1)}, bf16[1024,1,2,64]{0,3,2,1:T(8,128)(2,1)}, u32[]{:S(2)}) copy-start(bf16[1024,1,2,64]{0,3,2,1:T(8,128)(2,1)} %copy-done.4) | copy-start | bytes 786436
  561.8 174.9 %all-to-all-start.1 = ((bf16[128,1,9,2880]{3,2,1,0:T(8,128)(2,1)}), bf16[128,1,9,2880]{3,2,1,0:T(8,128)(2,1)}, u32[]{:S(2)}, u32[]{:S(2)}) async-start(bf16[128,1,9,2880]{3,2,1,0:T(8,128)(2,1)} %copy.62), calls=%async_computation.1 | async-start | bytes 24117248 | tf_op jit(solution)/shard_map/all_to_all | solution.py:228
  839.4 7.2 copy-start.2
Sparse Core Ops, SparseCore 0:
  9.7 36.5 all-gather.9
  48.0 35.4 all-gather.11
  85.7 86.7 all-gather.7
  247.8 94.1 reduce-scatter.3
where the time goes:
time: 867 us; the launch traced here: 855 us
  waiting for transfers between devices  254 us (29%)
  blocking collectives  236 us (27%)
  local copies, waits for them, and re-layouts  181 us (21%)
  matrix products  58.8 us (7%)
  other arithmetic  46.2 us (5%)
  loops' own time  34.8 us (4%)
  starting transfers between devices  29 us (3%)
  between operations  15 us (2%)
    all_to_all x1, waiting for transfers between devices, shards(): lax.all_to_all(produced, ('row', 'col'), split_axis=0, concat_axis=0, til...  161 us
    all_to_all x1, blocking collectives, shards(): lax.all_to_all(outgoing, ('row', 'col'), split_axis=0, concat_axis=0, til...  145 us
    reduce_scatter x1, waiting for transfers between devices, shards(): lax.psum_scatter(partial_value.astype(jnp.bfloat16), 'row', scatter_dimen...  88.8 us
    all_gather x1, blocking collectives, shards(): lax.all_gather(kv_weight, 'col', axis=0, tiled=True)  68.1 us
    another operation x1, loops' own time, entering(): return lax.fori_loop(0, place, one, state)  29.5 us
    convert_element_type x2, local copies, waits for them, and re-layouts, shards(): returned.reshape(EXPERTS, 2, CAP, feature_dim).astype(jnp.float32)  26.4 us
    unnamed x40, local copies, waits for them, and re-layouts  26 us
    reduce_sum x1, other arithmetic, shards(): jnp.sum(returned.reshape(EXPERTS, 2, CAP, feature_dim).astype(jnp.float32...  21.8 us
  transfers between devices with their start and end apart: 7, of which 3 were waited for; matrix products, arithmetic and copies ran while one was open for 5% of the time, Pallas kernels for 0%

commit v1 on v0

--- a/solution.py
+++ b/solution.py
@@ -3,6 +3,8 @@
 import jax
 import jax.numpy as jnp
 from jax import lax
+from jax.experimental import pallas as pl
+from jax.experimental.pallas import tpu as pltpu
 from jax.sharding import PartitionSpec as P
 
 HD = 64
@@ -96,17 +98,281 @@
     ).astype(jnp.bfloat16)
 
 
-def expert_block(arrived, expert_in, expert_out):
-    half_width = expert_out.shape[1]
-    mixed_in = jnp.einsum("nscd,sdf->nscf", arrived, expert_in, preferred_element_type=jnp.float32)
-    gate_part = mixed_in[..., :half_width]
-    up_part = mixed_in[..., half_width:]
-    hidden_act = (gate_part * jax.nn.sigmoid(glu_alpha * gate_part) * (up_part + 1.0)).astype(
-        jnp.bfloat16
-    )
-    return jnp.einsum(
-        "nscf,sfd->nscd", hidden_act, expert_out, preferred_element_type=jnp.float32
+def chip_place():
+    row, col = lax.axis_index("row"), lax.axis_index("col")
+    return (row // 4) * 2 + (col // 2) % 2, row % 4, col // 4, col % 2
+
+
+def device_at(x, y, z, core):
+    return ((x // 2) * 4 + y, z * 4 + (x % 2) * 2 + core)
+
+
+def expert_at(x, y, z):
+    return ((x // 2) * 4 + y) * 8 + z * 2 + x % 2
+
+
+def hop_order():
+    every = [(a, b, c) for a in range(4) for b in range(4) for c in range(4)]
+    reach = lambda v: sum(min(s, 4 - s) for s in v)
+    return sorted([v for v in every if v != (0, 0, 0)], key=lambda v: -reach(v))
+
+
+def exchange_kernel(out_msgs, in_msgs, send_sem, recv_sem, own_sem):
+    x, y, z, core = chip_place()
+    me = expert_at(x, y, z)
+    offsets = hop_order()
+    barrier = pltpu.get_barrier_semaphore()
+    for dx, dy, dz in offsets:
+        pl.semaphore_signal(
+            barrier,
+            inc=1,
+            device_id=device_at((x + dx) % 4, (y + dy) % 4, (z + dz) % 4, core),
+            device_id_type=pl.DeviceIdType.MESH,
+        )
+    own = pltpu.make_async_copy(out_msgs.at[me], in_msgs.at[me], own_sem)
+    own.start()
+    pl.semaphore_wait(barrier, len(offsets))
+    copies = []
+    for number, (dx, dy, dz) in enumerate(offsets):
+        there = ((x + dx) % 4, (y + dy) % 4, (z + dz) % 4)
+        copy = pltpu.make_async_remote_copy(
+            src_ref=out_msgs.at[expert_at(*there)],
+            dst_ref=in_msgs.at[me],
+            send_sem=send_sem.at[number],
+            recv_sem=recv_sem.at[number],
+            device_id=device_at(*there, core),
+            device_id_type=pl.DeviceIdType.MESH,
+        )
+        copy.start()
+        copies.append(copy)
+    own.wait()
+    for copy in copies:
+        copy.wait()
+
+
+def exchange(messages, ident, name):
+    others = EXPERTS - 1
+    return pl.pallas_call(
+        exchange_kernel,
+        out_shape=jax.ShapeDtypeStruct(messages.shape, messages.dtype),
+        in_specs=[pl.BlockSpec(memory_space=pl.ANY)],
+        out_specs=pl.BlockSpec(memory_space=pl.ANY),
+        scratch_shapes=[
+            pltpu.SemaphoreType.DMA((others,)),
+            pltpu.SemaphoreType.DMA((others,)),
+            pltpu.SemaphoreType.DMA,
+        ],
+        compiler_params=pltpu.CompilerParams(collective_id=ident, has_side_effects=True),
+        name=name,
+    )(messages)
+
+
+def slot_grid(routes_t, tokens_here):
+    expert_ids = lax.broadcasted_iota(jnp.int32, (EXPERTS, tokens_here), 0)
+    hit = jnp.zeros((EXPERTS, tokens_here), jnp.float32)
+    for j in range(TOP):
+        hit = hit + (routes_t[j : j + 1, :] == expert_ids).astype(jnp.float32)
+    earlier = (
+        lax.broadcasted_iota(jnp.int32, (tokens_here, tokens_here), 0)
+        < lax.broadcasted_iota(jnp.int32, (tokens_here, tokens_here), 1)
     ).astype(jnp.bfloat16)
+    rank = jnp.dot(hit.astype(jnp.bfloat16), earlier, preferred_element_type=jnp.float32)
+    return hit, rank
+
+
+def by_slot(hit, rank, amount):
+    tokens_here = hit.shape[1]
+    slot_ids = lax.broadcasted_iota(jnp.int32, (EXPERTS, 8, tokens_here), 1).astype(jnp.float32)
+    first = jnp.where(
+        (hit[:, None, :] > 0.5) & (rank[:, None, :] == slot_ids), amount[:, None, :], 0.0
+    ).reshape(EXPERTS * 8, tokens_here)
+    last = jnp.where((hit > 0.5) & (rank == 8.0), amount, 0.0)
+    return first, last
+
+
+def tiles_of(width):
+    return [(k, k * 128, min(128, width - k * 128)) for k in range(-(-width // 128))]
+
+
+def widen(tile):
+    short = 128 - tile.shape[1]
+    if short:
+        tile = jnp.concatenate([tile, jnp.zeros((tile.shape[0], short), tile.dtype)], axis=1)
+    return tile
+
+
+def pack_message(out_ref, last_ref, tile_first, tile_last, k):
+    out_ref[:, k] = widen(tile_first).reshape(EXPERTS, 8, 128).astype(jnp.bfloat16)
+    last_ref[pl.ds(k, EXPERTS, stride=24), :] = widen(tile_last)
+
+
+def finish_message(out_ref, last_ref, tile_count):
+    for k in range(tile_count, 24):
+        last_ref[pl.ds(k, EXPERTS, stride=24), :] = jnp.zeros((EXPERTS, 128), jnp.float32)
+    out_ref[:, tile_count:] = (
+        last_ref[...].reshape(EXPERTS, 3, 8, 128).astype(jnp.bfloat16)
+    )
+
+
+def unpack_last(in_ref, last_ref, tile_count):
+    last_ref[...] = in_ref[:, tile_count:].astype(jnp.float32).reshape(EXPERTS * 24, 128)
+
+
+def unpack_tile(in_ref, last_ref, k):
+    first = in_ref[:, k].astype(jnp.float32).reshape(EXPERTS * 8, 128)
+    last = last_ref[pl.ds(k, EXPERTS, stride=24), :]
+    return jnp.concatenate([first, last], axis=0).astype(jnp.bfloat16)
+
+
+def dispatch_kernel(tok_ref, add_ref, gain_ref, routes_ref, out_ref, last_ref):
+    hidden = tok_ref[...].astype(jnp.float32) + add_ref[...].astype(jnp.float32)
+    moe_in = rms_scale(hidden, gain_ref[...]).astype(jnp.bfloat16)
+    hit, rank = slot_grid(routes_ref[...], hidden.shape[0])
+    first, last = by_slot(hit, rank, jnp.ones_like(hit))
+    first, last = first.astype(jnp.bfloat16), last.astype(jnp.bfloat16)
+    tiles = tiles_of(hidden.shape[1])
+    for k, start, width in tiles:
+        piece = moe_in[:, start : start + width]
+        pack_message(
+            out_ref,
+            last_ref,
+            jnp.dot(first, piece, preferred_element_type=jnp.float32),
+            jnp.dot(last, piece, preferred_element_type=jnp.float32),
+            k,
+        )
+    finish_message(out_ref, last_ref, len(tiles))
+
+
+def combine_kernel(tok_ref, add_ref, routes_ref, weights_ref, in_ref, out_ref, last_ref):
+    routes_t, weights_t = routes_ref[...], weights_ref[...]
+    tokens_here = routes_t.shape[1]
+    hit, rank = slot_grid(routes_t, tokens_here)
+    expert_ids = lax.broadcasted_iota(jnp.int32, (EXPERTS, tokens_here), 0)
+    amount = jnp.zeros((EXPERTS, tokens_here), jnp.float32)
+    for j in range(TOP):
+        amount = amount + jnp.where(
+            routes_t[j : j + 1, :] == expert_ids, weights_t[j : j + 1, :], 0.0
+        )
+    mix = jnp.concatenate(by_slot(hit, rank, amount), axis=0).T
+    mix_high = mix.astype(jnp.bfloat16)
+    mix_low = (mix - mix_high.astype(jnp.float32)).astype(jnp.bfloat16)
+    tiles = tiles_of(out_ref.shape[1])
+    unpack_last(in_ref, last_ref, len(tiles))
+    for k, start, width in tiles:
+        rows = unpack_tile(in_ref, last_ref, k)
+        total = jnp.dot(mix_high, rows, preferred_element_type=jnp.float32) + jnp.dot(
+            mix_low, rows, preferred_element_type=jnp.float32
+        )
+        here = slice(start, start + width)
+        hidden = tok_ref[:, here].astype(jnp.float32) + add_ref[:, here].astype(jnp.float32)
+        out_ref[:, here] = (hidden + total[:, :width]).astype(jnp.bfloat16)
+
+
+def expert_kernel(
+    in_ref, gate_a, up_a, down_a, gate_b, up_b, down_b, out_ref, rows_ref, total_ref, last_ref
+):
+    half, step = pl.program_id(0), pl.program_id(1)
+    width = total_ref.shape[1]
+    tiles = tiles_of(width)
+
+    @pl.when((half == 0) & (step == 0))
+    def _():
+        unpack_last(in_ref, last_ref, len(tiles))
+        for k, start, wide in tiles:
+            rows_ref[:, start : start + wide] = unpack_tile(in_ref, last_ref, k)[:, :wide]
+
+    def run(gate, up, down, fresh):
+        rows = rows_ref[...]
+        gate_part = jnp.dot(rows, gate[0], preferred_element_type=jnp.float32)
+        up_part = jnp.dot(rows, up[0], preferred_element_type=jnp.float32)
+        act = (gate_part * jax.nn.sigmoid(glu_alpha * gate_part) * (up_part + 1.0)).astype(
+            jnp.bfloat16
+        )
+        part = lax.dot_general(
+            act, down[0], (((1,), (1,)), ((), ())), preferred_element_type=jnp.float32
+        )
+        if fresh:
+            total_ref[...] = part
+        else:
+            total_ref[...] += part
+
+    @pl.when((half == 0) & (step == 0))
+    def _():
+        run(gate_a, up_a, down_a, True)
+
+    @pl.when((half == 0) & (step != 0))
+    def _():
+        run(gate_a, up_a, down_a, False)
+
+    @pl.when(half == 1)
+    def _():
+        run(gate_b, up_b, down_b, False)
+
+    @pl.when((half == 1) & (step == pl.num_programs(1) - 1))
+    def _():
+        for k, start, wide in tiles:
+            tile = total_ref[:, start : start + wide]
+            pack_message(out_ref, last_ref, tile[: EXPERTS * 8], tile[EXPERTS * 8 :], k)
+        finish_message(out_ref, last_ref, len(tiles))
+
+
+def run_experts(arrived, own_in, own_out, peer_in, peer_out):
+    width, half_width = own_in.shape[1], own_out.shape[2]
+    chunk = 256
+    steps = half_width // chunk
+    first = lambda h, s: jnp.where(h == 0, s, steps - 1)
+    second = lambda h, s: jnp.where(h == 0, 0, s)
+    block_in, block_out = (1, width, chunk), (1, width, chunk)
+    specs = []
+    for pick in (first, second):
+        specs += [
+            pl.BlockSpec(block_in, lambda h, s, pick=pick: (0, 0, pick(h, s))),
+            pl.BlockSpec(block_in, lambda h, s, pick=pick: (0, 0, pick(h, s) + steps)),
+            pl.BlockSpec(block_out, lambda h, s, pick=pick: (0, 0, pick(h, s))),
+        ]
+    rows = EXPERTS * CAP
+    return pl.pallas_call(
+        expert_kernel,
+        grid=(2, steps),
+        out_shape=jax.ShapeDtypeStruct(arrived.shape, arrived.dtype),
+        in_specs=[pl.BlockSpec(memory_space=pltpu.VMEM)] + specs,
+        out_specs=pl.BlockSpec(memory_space=pltpu.VMEM),
+        scratch_shapes=[
+            pltpu.VMEM((rows, width), jnp.bfloat16),
+            pltpu.VMEM((rows, width), jnp.float32),
+            pltpu.VMEM((EXPERTS * 24, 128), jnp.float32),
+        ],
+        compiler_params=pltpu.CompilerParams(vmem_limit_bytes=60 * 2**20),
+        name="experts",
+    )(arrived, own_in, own_in, own_out, peer_in, peer_in, peer_out)
+
+
+def expert_layer(tokens, head_total, moe_gain, routes, route_weights, own, peer):
+    tokens_here, width = tokens.shape
+    vmem = pl.BlockSpec(memory_space=pltpu.VMEM)
+    message = jax.ShapeDtypeStruct((EXPERTS, -(-width // 128) + 3, 8, 128), jnp.bfloat16)
+    last = pltpu.VMEM((EXPERTS * 24, 128), jnp.float32)
+    outgoing = pl.pallas_call(
+        dispatch_kernel,
+        out_shape=message,
+        in_specs=[vmem] * 4,
+        out_specs=vmem,
+        scratch_shapes=[last],
+        compiler_params=pltpu.CompilerParams(vmem_limit_bytes=40 * 2**20),
+        name="dispatch",
+    )(tokens, head_total, moe_gain.reshape(1, width), routes.T)
+    arrived = exchange(outgoing, 1, "exchange_out")
+    produced = run_experts(arrived, *own, *peer)
+    returned = exchange(produced, 2, "exchange_back")
+    return pl.pallas_call(
+        combine_kernel,
+        out_shape=jax.ShapeDtypeStruct((tokens_here, width), jnp.bfloat16),
+        in_specs=[vmem] * 5,
+        out_specs=vmem,
+        scratch_shapes=[last],
+        compiler_params=pltpu.CompilerParams(vmem_limit_bytes=40 * 2**20),
+        name="combine",
+    )(tokens, head_total, routes.T, route_weights.T, returned)
 
 
 def shards(
@@ -123,7 +389,9 @@
     expert_in,
     expert_out,
 ):
-    feature_dim = tokens.shape[1]
+    swap = [(c, c + 1 - 2 * (c % 2)) for c in range(lax.axis_size("col"))]
+    own_in, own_out = expert_in, jnp.swapaxes(expert_out, 1, 2)
+    peer_in, peer_out = (lax.ppermute(w, "col", swap) for w in (own_in, own_out))
     normed = rms_scale(tokens, norm_gain).astype(jnp.bfloat16)
     block_x, block_seg = (
         lax.all_gather(normed, "row", axis=0, tiled=True),
@@ -199,39 +467,10 @@
     )
     head_total = lax.psum_scatter(
         partial_value.astype(jnp.bfloat16), "row", scatter_dimension=0, tiled=True
-    ).astype(jnp.float32)
-    hidden = tokens.astype(jnp.float32) + head_total
-    moe_in = rms_scale(hidden, moe_gain).astype(jnp.bfloat16)
-    route_flat = routes.reshape(-1)
-    route_count = route_flat.shape[0]
-    expert_ids = jnp.arange(EXPERTS, dtype=jnp.int32)
-    hit_table = (route_flat[:, None] == expert_ids[None, :]).astype(jnp.int32)
-    slot_ranks = jnp.sum((jnp.cumsum(hit_table, axis=0) - hit_table) * hit_table, axis=1)
-    slot_index = route_flat * CAP + slot_ranks
-    slot_table = (
-        jnp.full((EXPERTS * CAP,), route_count, jnp.int32)
-        .at[slot_index]
-        .set(jnp.arange(route_count, dtype=jnp.int32))
-    )
-    padded_rows = jnp.concatenate([moe_in, jnp.zeros((1, feature_dim), jnp.bfloat16)], axis=0)
-    outgoing = padded_rows[slot_table // TOP]
-    outgoing = jnp.broadcast_to(
-        outgoing.reshape(EXPERTS, 1, CAP, feature_dim), (EXPERTS, 2, CAP, feature_dim)
-    )
-    slices_here = expert_in.shape[0]
-    row_count = lax.axis_size("row")
-    col_count = lax.axis_size("col")
-    device_count = row_count * col_count
-    outgoing = outgoing.reshape(device_count, slices_here, CAP, feature_dim)
-    arrived = lax.all_to_all(outgoing, ("row", "col"), split_axis=0, concat_axis=0, tiled=True)
-    produced = expert_block(arrived, expert_in, expert_out)
-    returned = lax.all_to_all(produced, ("row", "col"), split_axis=0, concat_axis=0, tiled=True)
-    combined = jnp.sum(
-        returned.reshape(EXPERTS, 2, CAP, feature_dim).astype(jnp.float32), axis=1
-    ).reshape(EXPERTS * CAP, feature_dim)
-    weighted = combined[slot_index] * route_weights.reshape(-1)[:, None]
-    expert_total = jnp.sum(weighted.reshape(-1, TOP, feature_dim), axis=1)
-    mixed = (hidden + expert_total).astype(jnp.bfloat16)
+    )
+    mixed = expert_layer(
+        tokens, head_total, moe_gain, routes, route_weights, (own_in, own_out), (peer_in, peer_out)
+    )
     return (mixed, kv_cache)
 
 

time: 867 us -> 492 us (0.57)
  the two profiles are of different devices: /device:TPU:51 before, /device:TPU:2 now
where the time goes in v1:
time: 492 us; the launch traced here: 483 us
  blocking collectives  140 us (28%)
  Pallas kernels  138 us (28%)
  waiting for transfers between devices  94.3 us (19%)
  local copies, waits for them, and re-layouts  37.5 us (8%)
  matrix products  25.2 us (5%)
  loops' own time  14.7 us (3%)
  between operations  14.7 us (3%)
  other arithmetic  14.6 us (3%)
  starting transfers between devices  5.22 us (1%)
    all_gather x1, blocking collectives, shards(): lax.all_gather(kv_weight, 'col', axis=0, tiled=True)  103 us
    pallas_call x2, Pallas kernels, exchange(): pl.pallas_call(exchange_kernel, out_shape=jax.ShapeDtypeStruct(messages.s...  99.5 us
    reduce_scatter x1, waiting for transfers between devices, shards(): lax.psum_scatter(partial_value.astype(jnp.bfloat16), 'row', scatter_dimen...  91.8 us
    pallas_call x1, Pallas kernels, run_experts(): pl.pallas_call(expert_kernel, grid=(2, steps), out_shape=jax.ShapeDtypeSt...  34 us
    all_gather x1, blocking collectives, shards(): lax.all_gather(seg_ids, 'row', axis=0, tiled=True)  22.8 us
    unnamed x35, local copies, waits for them, and re-layouts  20.4 us
    unnamed x1, blocking collectives  13.7 us
  transfers between devices with their start and end apart: 8, of which 2 were waited for; matrix products, arithmetic and copies ran while one was open for 5% of the time, Pallas kernels for 10%

profile of v1, /device:TPU:2, one launch (start us, length us, event | category | flops | bytes accessed | tf_op | source)
XLA Modules:
  0.0 483.4 jit_solution(2977124926461063629)
XLA Ops:
  7.2 0.7 all-gather.10.cloned.1.call-update
  7.9 0.7 all-gather.12.cloned.1.call-update
  8.7 1.5 fusion.17
  10.2 2.4 fusion.19
  12.7 22.8 %all-gather.1 = s32[8,1,128]{2,1,0:T(1,128)S(1)} all-gather(s32[1,1,128]{2,1,0:T(1,128)} %bitcast.132), channel_id=1, replica_groups=mesh['row'=8,'col'=16] {'row'}, dimensions={0}, use_global_device_ids=true | all-gather | bytes 4608 | tf_op jit(solution)/shard_map/all_gather | solution.py:398
  35.6 1.9 collective-permute-start.1
  37.5 1.2 dynamic-slice
  38.7 1.2 slice_dynamic-update-slice_fusion.2
  40.9 0.8 slice_dynamic-update-slice_fusion.1
  41.9 0.8 slice_dynamic-update-slice_fusion
  42.8 13.7 %all-reduce.3 = (s32[16]{0:T(128)S(1)}, s32[16]{0:T(128)S(1)}, s32[16]{0:T(128)S(1)}) all-reduce(s32[16]{0:T(128)S(1)} %slice_dynamic-update-slice_fusion.1, s32[16]{0:T(128)S(1)} %get-tuple-element.201, s32[16]{0:T(128)S(1)} %slice_dynamic-update-slice_fusion), channel_id=1, replica_groups=mesh['row'=8,'col'=16] {'col'}, use_global_device_ids=true, to_apply=%add | all-reduce | flops 48 | bytes 384
  56.5 13.1 %while.24 = (s32[]{:T(128)}, s32[]{:T(128)}, s32[]{:T(128)}, s32[]{:T(128)}, s32[16]{0:T(128)S(1)}, /*index=5*/s32[16]{0:T(128)S(1)}, s32[16]{0:T(128)S(1)}, s32[]{:T(128)}, s32[]{:T(128)}, s32[]{:T(128)}) while((s32[]{:T(128)}, s32[]{:T(128)}, s32[]{:T(128)}, s32[]{:T(128)}, s32[16]{0:T(128)S(1)}, /*index=5*/s32[16]{0:T(128)S(1)}, ...), condition=%wide.region_4.5_spmd, body=%wide.region_3.4_spmd.sunk | while | flops 13 | bytes 255 | solution.py:33
  58.4 0.7 dynamic_slice.53
  65.0 0.7 dynamic_slice.53
  70.2 1.2 multiply_cosine_fusion
  71.4 103.2 %all-gather = bf16[16,180,128]{2,1,0:T(8,128)(2,1)S(1)} all-gather(bf16[1,180,128]{2,1,0:T(8,128)(2,1)} %bitcast.129), channel_id=1, replica_groups=mesh['row'=8,'col'=16] {'col'}, dimensions={0}, use_global_device_ids=true | all-gather | bytes 783360 | tf_op jit(solution)/shard_map/all_gather | solution.py:419
  174.6 1.0 reshape.418
  175.6 2.8 reshape.422
  178.5 4.3 reshape.424
  182.8 4.0 fusion.32
  187.4 3.4 fusion.33
  192.6 2.6 collective-permute-start
  195.2 1.4 pad_maximum_fusion
  196.7 1.1 collective-permute-done
  197.9 24.9 %while.25 = (s32[]{:T(128)}, bf16[2,512,512]{2,1,0:T(8,128)(2,1)}, s32[2]{0:T(128)S(1)}, bf16[1152,1,2,64]{0,3,2,1:T(8,128)(2,1)S(1)}, s32[1024]{0:T(1024)S(1)},...) while((s32[]{:T(128)}, bf16[2,512,512]{2,1,0:T(8,128)(2,1)}, ...), condition=%wide.region_8.9_spmd, body=%wide.region_5.8_spmd.sunk | while | flops 705110656 | bytes 36270728 | solution.py:460
  201.4 0.7 fusion.46
  202.1 1.8 fusion.47
  203.9 2.1 fusion.48
  206.1 3.1 fusion.49
  209.5 0.8 constant_dynamic-update-slice_fusion.2
  213.8 0.7 fusion.46
  214.5 1.8 fusion.47
  216.3 2.1 fusion.48
  218.5 3.1 fusion.49
  221.9 0.9 constant_dynamic-update-slice_fusion.2
  222.8 8.0 %convolution_convert_fusion = bf16[1024,2880]{0,1:T(8,128)(2,1)} fusion(bf16[1024,512]{1,0:T(8,128)(2,1)} %bitcast.133, bf16[2880,512]{1,0:T(8,128)(2,1)} %reshape.424), kind=kOutput, calls=%fused_computation.26 | convolution fusion | flops 3022848000 | bytes 9895936 | tf_op jit(solution)/shard_map/dot_general | solution.py:463
  230.7 8.5 %copy.39 = bf16[1024,2880]{1,0:T(8,128)(2,1)} copy(bf16[1024,2880]{0,1:T(8,128)(2,1)} %convolution_convert_fusion) | data formatting | bytes 11796480 | tf_op jit(solution)/shard_map/convert_element_type | solution.py:469
  240.7 0.8 copy.43
  241.5 91.8 %reduce-scatter.2.cloned.1.call-done.add_ref = bf16[128,2880]{1,0:T(8,128)(2,1)} async-done(((bf16[1024,2880]{1,0:T(8,128)(2,1)}), bf16[128,2880]{1,0:T(8,128)(2,1)}) %reduce-scatter.2.cloned.1.call-update) | async-done | bytes 737296 | tf_op jit(solution)/shard_map/reduce_scatter | solution.py:468
  333.3 1.1 copy-done.2
  334.5 1.6 dispatch.1.out_msgs
  336.1 1.7 copy-done.1
  337.8 48.8 %exchange_out.1.in_ref = bf16[64,26,8,128]{3,2,1,0:T(8,128)(2,1)} custom-call(bf16[64,26,8,128]{3,2,1,0:T(8,128)(2,1)} %copy-done.1), custom_call_target="tpu_custom_call" | custom-call | tf_op jit(solution)/shard_map/exchange_out/pallas_call | solution.py:155
  386.6 34.0 %experts.1.out_msgs = bf16[64,26,8,128]{3,2,1,0:T(8,128)(2,1)} custom-call(bf16[64,26,8,128]{3,2,1,0:T(8,128)(2,1)} %exchange_out.1.in_ref, bf16[1,2880,1536]{2,1,0:T(8,128)(2,1)} %up_a.1, bf16[1,2880,1536]{2,1,0:T(8,128)(2,1)} %up_a.1, bf16[1,2880,768]{2,1,0:T(8,128)(2,1)} %bitcast.116, bf16[1,2880,1536]{2,1,0:T(8,128)(2,1)} %collective-permute-done.2.gate_b.up_b, ...), custom_call_target="tpu_custom_call" | custom-call | tf_op jit(solution)/shard_map/experts/pallas_call | solution.py:334
  420.6 50.7 %exchange_back.1.in_ref = bf16[64,26,8,128]{3,2,1,0:T(8,128)(2,1)} custom-call(bf16[64,26,8,128]{3,2,1,0:T(8,128)(2,1)} %experts.1.out_msgs), custom_call_target="tpu_custom_call" | custom-call | tf_op jit(solution)/shard_map/exchange_back/pallas_call | solution.py:155
  471.4 2.0 copy-done
  473.3 2.4 combine.1
  475.7 1.2 copy.42
  (83 shorter events, 10.2 us)
Async XLA Ops:
  7.2 168.5 %all-gather.10.cloned.1.call-start = ((), (), s32[]{:S(2)}) async-start(), calls=%async_computation.3 | async-start | bytes 3203072 | tf_op jit(solution)/shard_map/all_gather | solution.py:414
  7.9 170.6 %all-gather.12.cloned.1.call-start = ((), (), s32[]{:S(2)}) async-start(), calls=%async_computation.4 | async-start | bytes 3203072 | tf_op jit(solution)/shard_map/all_gather | solution.py:465
  8.6 174.2 %all-gather.8.cloned.1.call-start = ((), (), s32[]{:S(2)}) async-start(), calls=%async_computation.1 | async-start | bytes 6635520 | tf_op jit(solution)/shard_map/all_gather | solution.py:397
  12.7 320.7 %reduce-scatter.2.cloned.1.call-start = ((), (), s32[]{:S(2)}) async-start(), calls=%async_computation.2 | async-start | bytes 6782976 | tf_op jit(solution)/shard_map/reduce_scatter | solution.py:468
  35.6 140.0 %collective-permute-start.1 = (s32[128]{0:T(128)S(1)}, s32[128]{0:T(128)S(1)}, u32[]{:S(2)}, u32[]{:S(2)}) collective-permute-start(s32[128]{0:T(128)S(1)} %slice_bitcast_fusion.1), channel_id=1, source_target_pairs={{0,1},{1,2},{2,3},{3,4},{4,5},{5,6},{6,7},{7,8},{8,9},{9,10},{10,1... | collective-permute-start | bytes 1544 | tf_op jit(solution)/shard_map/ppermute | solution.py:39
  182.8 4.6 copy-start.10
  187.4 3.5 copy-start.7
  190.9 7.0 %copy-start.8 = (f32[8]{0:T(128)S(1)}, f32[8]{0:T(128)}, u32[]{:S(2)}) copy-start(f32[8]{0:T(128)} %param.22) | copy-start | bytes 100
  192.6 5.2 %collective-permute-start = (bf16[128,128]{0,1:T(8,128)(2,1)S(1)}, bf16[128,128]{0,1:T(8,128)(2,1)S(1)}, u32[]{:S(2)}, u32[]{:S(2)}) collective-permute-start(bf16[128,128]{0,1:T(8,128)(2,1)S(1)} %bitcast.131), channel_id=1, source_target_pairs={{0,1},{1,2},{2,3},{3,4},{4,5},{5,6},{6,7},{7,8},{8,9},{9,10},{10,1... | collective-permute-start | bytes 98312 | tf_op jit(solution)/shard_map/ppermute | solution.py:39
  239.2 1.1 copy-start.6
  239.2 1.5 copy-start.9
  239.2 94.1 %copy-start.4 = (s32[128,4]{0,1:T(4,128)S(1)}, s32[128,4]{0,1:T(4,128)}, u32[]{:S(2)}) copy-start(s32[128,4]{0,1:T(4,128)} %param.24) | copy-start | bytes 6148
  239.2 147.4 %collective-permute-start.2 = (bf16[1,2880,1536]{2,1,0:T(8,128)(2,1)}, bf16[1,2880,1536]{2,1,0:T(8,128)(2,1)}, u32[]{:S(2)}, u32[]{:S(2)}) collective-permute-start(bf16[1,2880,1536]{2,1,0:T(8,128)(2,1)} %up_a.1), channel_id=1, source_target_pairs={{0,1},{1,0},{2,3},{3,2},{4,5},{5,4},{6,7},{7,6},{8,9},{9,8},{10,11... | collective-permute-start | bytes 26542088 | tf_op jit(solution)/shard_map/ppermute | solution.py:394
  239.3 147.3 %collective-permute-start.3 = (bf16[1,2880,768]{2,1,0:T(8,128)(2,1)}, bf16[1,2880,768]{2,1,0:T(8,128)(2,1)}, u32[]{:S(2)}, u32[]{:S(2)}) collective-permute-start(bf16[1,2880,768]{2,1,0:T(8,128)(2,1)} %bitcast.115), channel_id=1, source_target_pairs={{0,1},{1,0},{2,3},{3,2},{4,5},{5,4},{6,7},{7,6},{8,9},{9,8},{10,11... | collective-permute-start | bytes 13271048 | tf_op jit(solution)/shard_map/ppermute | solution.py:394
  333.3 1.1 copy-start.2
  336.1 1.7 copy-start.1
  420.6 50.7 %copy-start.3 = (bf16[128,2880]{1,0:T(8,128)(2,1)S(1)}, bf16[128,2880]{1,0:T(8,128)(2,1)}, u32[]{:S(2)}) copy-start(bf16[128,2880]{1,0:T(8,128)(2,1)} %reduce-scatter.2.cloned.1.call-done.add_ref) | copy-start | bytes 2211844
  420.6 50.7 %copy-start.5 = (f32[128,4]{0,1:T(4,128)S(1)}, f32[128,4]{0,1:T(4,128)}, u32[]{:S(2)}) copy-start(f32[128,4]{0,1:T(4,128)} %param.25) | copy-start | bytes 6148
  471.4 2.0 copy-start
Sparse Core Ops, SparseCore 0:
  9.7 37.4 all-gather.9
  48.9 35.3 all-gather.11
  87.0 91.9 all-gather.7
  239.4 93.9 reduce-scatter.1

commit v2 on v1

v2 whole, which is shorter than its diff:
```python
import functools
import math

import jax
import jax.numpy as jnp
from jax import lax
from jax.experimental import pallas as pl
from jax.experimental.pallas import tpu as pltpu
from jax.sharding import PartitionSpec as P

HD = 64
WIN = 128
EXPERTS = 64
TOP = 4
CAP = 9
SEGS = 16


eps_norm = 1e-05
theta_base = 150000.0
glu_alpha = 1.702
masked_score = -1e30


def rms_scale(widened, gain_vec, width):
    mean_square = jnp.sum(widened * widened, axis=-1, keepdims=True) * (1.0 / width)
    return widened * lax.rsqrt(mean_square + eps_norm) * gain_vec


def chip_place():
    row, col = lax.axis_index("row"), lax.axis_index("col")
    return (row // 4) * 2 + (col // 2) % 2, row % 4, col // 4, col % 2


def device_at(x, y, z, core):
    return ((x // 2) * 4 + y, z * 4 + (x % 2) * 2 + core)


def expert_at(x, y, z):
    return ((x // 2) * 4 + y) * 8 + z * 2 + x % 2


def hop_order():
    every = [(a, b, c) for a in range(4) for b in range(4) for c in range(4)]
    reach = lambda v: sum(min(s, 4 - s) for s in v)
    return sorted([v for v in every if v != (0, 0, 0)], key=lambda v: -reach(v))


def exchange_kernel(out_msgs, in_msgs, send_sem, recv_sem, own_sem):
    x, y, z, core = chip_place()
    me = expert_at(x, y, z)
    offsets = hop_order()
    barrier = pltpu.get_barrier_semaphore()
    for dx, dy, dz in offsets:
        pl.semaphore_signal(
            barrier,
            inc=1,
            device_id=device_at((x + dx) % 4, (y + dy) % 4, (z + dz) % 4, core),
            device_id_type=pl.DeviceIdType.MESH,
        )
    own = pltpu.make_async_copy(out_msgs.at[me], in_msgs.at[me], own_sem)
    own.start()
    pl.semaphore_wait(barrier, len(offsets))
    copies = []
    for number, (dx, dy, dz) in enumerate(offsets):
        there = ((x + dx) % 4, (y + dy) % 4, (z + dz) % 4)
        copy = pltpu.make_async_remote_copy(
            src_ref=out_msgs.at[expert_at(*there)],
            dst_ref=in_msgs.at[me],
            send_sem=send_sem.at[number],
            recv_sem=recv_sem.at[number],
            device_id=device_at(*there, core),
            device_id_type=pl.DeviceIdType.MESH,
        )
        copy.start()
        copies.append(copy)
    own.wait()
    for copy in copies:
        copy.wait()


def exchange(messages, ident, name):
    others = EXPERTS - 1
    return pl.pallas_call(
        exchange_kernel,
        out_shape=jax.ShapeDtypeStruct(messages.shape, messages.dtype),
        in_specs=[pl.BlockSpec(memory_space=pl.ANY)],
        out_specs=pl.BlockSpec(memory_space=pl.ANY),
        scratch_shapes=[
            pltpu.SemaphoreType.DMA((others,)),
            pltpu.SemaphoreType.DMA((others,)),
            pltpu.SemaphoreType.DMA,
        ],
        compiler_params=pltpu.CompilerParams(collective_id=ident, has_side_effects=True),
        name=name,
    )(messages)


def send(source, target, sems, number, device):
    copy = pltpu.make_async_remote_copy(
        src_ref=source,
        dst_ref=target,
        send_sem=sems[0].at[number],
        recv_sem=sems[1].at[number],
        device_id=device,
        device_id_type=pl.DeviceIdType.MESH,
    )
    copy.start()
    return copy


def greet(devices):
    barrier = pltpu.get_barrier_semaphore()
    for device in devices:
        pl.semaphore_signal(
            barrier, inc=1, device_id=device, device_id_type=pl.DeviceIdType.MESH
        )
    pl.semaphore_wait(barrier, len(devices))


class Ring:
    def __init__(self, own, place, device, sems, first):
        self.place, self.device, self.sems, self.first = place, device, sems, first
        self.sent = [
            self.pass_on(0, own(0), 0, 0, 1),
            self.pass_on(1, own(1), 0, 1, 1),
            self.pass_on(2, own(1), 0, 1, 3),
            self.pass_on(3, own(0), 0, 0, 3),
        ]

    def pass_on(self, number, source, owner, half, to):
        return send(
            source, self.place(owner, half), self.sems, self.first + number, self.device(to)
        )

    def take_left(self):
        self.sent[0].wait_recv()
        self.sent.append(self.pass_on(4, self.place(3, 0), 3, 0, 1))
        self.sent[1].wait_recv()

    def take_right(self):
        self.sent[2].wait_recv()
        self.sent.append(self.pass_on(5, self.place(1, 1), 1, 1, 3))
        self.sent[3].wait_recv()

    def take_far(self):
        self.sent[4].wait_recv()
        self.sent[5].wait_recv()

    def close(self):
        for copy in self.sent:
            copy.wait_send()


SHARD_CUT = 96


def gather_kernel(
    width,
    xt_ref,
    gain_ref,
    seg_ref,
    freq_ref,
    shard_ref,
    x_all,
    w_all,
    cos_ref,
    sin_ref,
    pos_ref,
    normed_ref,
    window_ref,
    send_sem,
    recv_sem,
    own_sem,
):
    x, y, z, core = chip_place()
    sems = (send_sem, recv_sem)
    run = lax.axis_index("col") * 2 + x // 2
    runs = 2 * lax.axis_size("col")
    shard_rows, shard_cols = shard_ref.shape

    def at(first, second):
        return (
            (x + first * core + second * (1 - core)) % 4,
            (z + first * (1 - core) + second * core) % 4,
        )

    def chip(first, second):
        there_x, there_z = at(first, second)
        return device_at(there_x, y, there_z, core)

    def run_device(steps):
        there = (run + steps + runs) % runs
        return ((there % 2) * 4 + y, there // 2)

    def y_device(steps):
        return device_at(x, (y + steps) % 4, z, core)

    sister = device_at(x, y, z, 1 - core)
    greet(
        [y_device(s) for s in (1, 2, 3)]
        + [chip(s, 0) for s in (1, 3)]
        + [chip(0, s) for s in (1, 3)]
        + [sister]
        + [run_device(s) for s in (1, 2, 3, 4, -1, -2, -3, -4)]
    )

    def half_rows(half):
        return pl.ds(0, SHARD_CUT) if half == 0 else pl.ds(SHARD_CUT, shard_rows - SHARD_CUT)

    def w_place(first, second, rows):
        there_x, there_z = at(first, second)
        lanes = pl.multiple_of((there_x // 2) * shard_cols, 128)
        return w_all.at[there_z * 4 + (there_x % 2) * 2 + core, rows, pl.ds(lanes, shard_cols)]

    own_seg = pltpu.make_async_copy(seg_ref, window_ref.at[0, y], own_sem.at[0])
    own_seg.start()
    seg_sent = [
        send(seg_ref, window_ref.at[0, y], sems, n, y_device(s)) for n, s in enumerate((1, 2, 3))
    ]

    every_row = pl.ds(0, shard_rows)
    own_w = pltpu.make_async_copy(shard_ref, w_place(0, 0, every_row), own_sem.at[1])
    own_w.start()
    own_half = lambda half: shard_ref.at[half_rows(half)]
    along = Ring(
        own_half, lambda o, h: w_place(o, 0, half_rows(h)), lambda s: chip(s, 0), sems, 8
    )

    def across(owner, number):
        own = own_half if owner == 0 else (lambda h: w_place(owner, 0, half_rows(h)))
        return Ring(
            own,
            lambda o, h: w_place(owner, o, half_rows(h)),
            lambda s: chip(0, s),
            sems,
            14 + 6 * number,
        )

    to_sister = []

    def hand_over(first, second):
        place = w_place(first, second, every_row)
        source = shard_ref if (first, second) == (0, 0) else place
        to_sister.append(send(source, place, sems, 38 + len(to_sister), sister))

    rings = [across(0, 0)]
    hand_over(0, 0)

    raw = xt_ref[...].astype(jnp.float32).T
    mean_square = jnp.sum(raw * raw, axis=1, keepdims=True) * (1.0 / width)
    normed_ref[...] = (raw * lax.rsqrt(mean_square + eps_norm) * gain_ref[...]).astype(jnp.bfloat16)

    own_seg.wait()
    for copy in seg_sent:
        copy.wait_recv()
    seg_on = [
        send(window_ref.at[0], window_ref.at[s], sems, 2 + s, run_device(s)) for s in (1, 2, 3, 4)
    ]

    rows_x = normed_ref.shape[0] // 2
    x_place = lambda o, h: x_all.at[(y + o) % 4, pl.ds(h * rows_x, rows_x)]
    own_x = pltpu.make_async_copy(normed_ref, x_all.at[y], own_sem.at[2])
    own_x.start()
    tokens_ring = Ring(
        lambda h: normed_ref.at[pl.ds(h * rows_x, rows_x)], x_place, y_device, sems, 54
    )

    along.take_left()
    rings.append(across(3, 1))
    hand_over(3, 0)
    along.take_right()
    rings.append(across(1, 2))
    hand_over(1, 0)
    rings[0].take_left()
    rings[0].take_right()
    tokens_ring.take_left()
    tokens_ring.take_right()
    along.take_far()
    rings.append(across(2, 3))
    hand_over(2, 0)
    owners = (0, 3, 1, 2)
    for number, owner in enumerate(owners):
        if number:
            rings[number].take_left()
        hand_over(owner, 3)
        if number:
            rings[number].take_right()
        hand_over(owner, 1)
        if number == 0:
            for copy in seg_on:
                copy.wait_recv()
            fill_tables(run, window_ref, freq_ref, cos_ref, sin_ref, pos_ref)
    for number, owner in enumerate(owners):
        rings[number].take_far()
        hand_over(owner, 2)
    tokens_ring.take_far()
    own_w.wait()
    own_x.wait()
    for copy in to_sister:
        copy.wait()
    for ring in [along, tokens_ring] + rings:
        ring.close()
    for copy in seg_sent + seg_on:
        copy.wait_send()


def fill_tables(run, window_ref, freq_ref, cos_ref, sin_ref, pos_ref):
    span, parts, _, lanes = window_ref.shape
    ids = [
        jnp.where(run - s >= 0, window_ref[s].reshape(parts * 8, lanes), -1).astype(jnp.float32)
        for s in range(span)
    ]
    ids = jnp.concatenate(ids, axis=0)
    fewer = [
        jnp.sum((ids < float(s)).astype(jnp.float32), keepdims=True) * 0.125 for s in range(SEGS)
    ]
    lane = lax.broadcasted_iota(jnp.int32, (lanes, lanes), 1)
    row = lax.broadcasted_iota(jnp.int32, (lanes, lanes), 0).astype(jnp.float32)
    for part in range(parts):
        own = window_ref[0, part].astype(jnp.float32)
        own = jnp.broadcast_to(own[0:1, :], (lanes, lanes)).T
        start = jnp.zeros((lanes, lanes), jnp.float32)
        for s in range(SEGS):
            start = jnp.where(own == float(s), fewer[s], start)
        position = row + float((span - 1) * parts * lanes + part * lanes) - start
        angle = position * freq_ref[...]
        turns = jnp.floor(angle * (0.5 / math.pi) + 0.5)
        angle = (angle - turns * 6.28125) - turns * (2.0 * math.pi - 6.28125)
        sine = jnp.sin(angle)
        here = pl.ds(part * lanes, lanes)
        cos_ref[here, :] = jnp.cos(angle)
        sin_ref[here, :] = jnp.where(lane % HD < HD // 2, -sine, sine)
        pos_ref[here, :] = position


def turned(tile, cosine, sine):
    lane = lax.broadcasted_iota(jnp.int32, tile.shape, 1)
    other = jnp.where(
        lane % HD < HD // 2, pltpu.roll(tile, 128 - HD // 2, 1), pltpu.roll(tile, HD // 2, 1)
    )
    return tile * cosine + other * sine


def attention_kernel(
    x_all,
    w_all,
    cos_ref,
    sin_ref,
    pos_ref,
    parts,
    kv_out,
    x_ref,
    w_ref,
    query_ref,
    kv_ref,
    sum_ref,
    send_sem,
    recv_sem,
    own_sem,
):
    x, y, z, core = chip_place()
    half = x // 2
    sems = (send_sem, recv_sem)
    run = lax.axis_index("col") * 2 + half
    runs = 2 * lax.axis_size("col")
    blocks, rows, padded = x_ref.shape

    def run_device(steps):
        there = (run + steps + runs) % runs
        return ((there % 2) * 4 + y, there // 2)

    def y_device(steps):
        return device_at(x, (y + steps) % 4, z, core)

    loads = [pltpu.make_async_copy(x_all, x_ref, own_sem.at[0])]
    query_cols = query_ref.shape[1] // 2
    shard_cols = w_ref.shape[1] // 2
    for h in range(2):
        lanes = pl.ds(h * shard_cols, query_cols + 2 * HD)
        loads.append(
            pltpu.make_async_copy(w_all.at[:, lanes], w_ref.at[:, lanes], own_sem.at[1 + h])
        )
    for h in range(2):
        lanes = pl.ds(h * shard_cols + query_cols + 2 * HD, query_cols)
        loads.append(
            pltpu.make_async_copy(w_all.at[:, lanes], w_ref.at[:, lanes], own_sem.at[3 + h])
        )
    for load in loads:
        load.start()
    partner = device_at((x + 2) % 4, y, z, core)
    greet([y_device(s) for s in (1, 2, 3)] + [run_device(1), run_device(-1), partner])

    loads[0].wait()
    cosine, sine = cos_ref[...], sin_ref[...]
    lane = lax.broadcasted_iota(jnp.int32, cosine.shape, 1)
    every = blocks * rows
    source = x_ref[...].reshape(every, padded)
    for h in range(2):
        loads[1 + h].wait()
        first = h * shard_cols
        mixed_kv = jnp.dot(
            source,
            w_ref[:, first : first + query_cols + 2 * HD],
            preferred_element_type=jnp.float32,
        )
        kv = mixed_kv[:, query_cols:]
        kv = jnp.where(lane < HD, turned(kv, cosine, sine), kv)
        kv_ref[h, pl.ds(rows, every), :] = kv.astype(jnp.bfloat16)
        for k in range(query_cols // 128):
            tile = turned(mixed_kv[:, k * 128 : k * 128 + 128], cosine, sine)
            query_ref[:, h * query_cols + k * 128 : h * query_cols + k * 128 + 128] = (
                tile * HD**-0.5
            ).astype(jnp.bfloat16)
    edge = send(
        kv_ref.at[:, pl.ds(every, rows)], kv_ref.at[:, pl.ds(0, rows)], sems, 0, run_device(1)
    )
    mine = pl.ds(pl.multiple_of(half * every, every), every)
    cache_there = send(
        kv_ref.at[1 - half, pl.ds(rows, every)], kv_out.at[mine], sems, 1, partner
    )
    cache_here = pltpu.make_async_copy(
        kv_ref.at[half, pl.ds(rows, every)], kv_out.at[mine], own_sem.at[5]
    )
    cache_here.start()
    loads[3].wait()
    loads[4].wait()
    edge.wait_recv()
    heads = query_cols // HD
    distance = (
        rows
        + lax.broadcasted_iota(jnp.int32, (rows, 2 * rows), 0)
        - lax.broadcasted_iota(jnp.int32, (rows, 2 * rows), 1)
    ).astype(jnp.float32)

    def out_copy(step, block):
        return pltpu.make_async_remote_copy(
            src_ref=sum_ref.at[step],
            dst_ref=parts.at[y],
            send_sem=send_sem.at[2 + step],
            recv_sem=recv_sem.at[2 + step],
            device_id=device_at(x, block, z, core),
            device_id_type=pl.DeviceIdType.MESH,
        )

    def one_block(step, carry):
        block = (y + 3 - step) % 4
        here = pl.ds(pl.multiple_of(block * rows, rows), rows)
        position = pos_ref[here, :]
        position = jnp.concatenate([position, position], axis=1)
        allowed = (distance >= 0) & (distance < WIN) & (distance <= position)
        allowed = jnp.concatenate([allowed.astype(jnp.float32)] * heads, axis=0) > 0.5
        total = None
        for h in range(2):
            first = h * shard_cols
            keys = kv_ref[h, pl.ds(pl.multiple_of(block * rows, rows), 2 * rows), :]
            values = jnp.where(
                lax.broadcasted_iota(jnp.int32, keys.shape, 1) < HD,
                pltpu.roll(keys.astype(jnp.float32), HD, 1),
                1.0,
            ).astype(jnp.bfloat16)
            query = query_ref[here, h * query_cols : (h + 1) * query_cols]
            query = jnp.concatenate(
                [query[:, n * HD : (n + 1) * HD] for n in range(heads)], axis=0
            )
            scores = lax.dot_general(
                query,
                keys[:, :HD],
                (((1,), (1,)), ((), ())),
                preferred_element_type=jnp.float32,
            )
            scores = jnp.where(allowed, scores, masked_score)
            sink_rows = w_ref[176:184, first : first + 128].astype(jnp.float32)
            sink_row = jnp.sum(sink_rows[4:8], axis=0, keepdims=True)
            sink = jnp.concatenate(
                [jnp.broadcast_to(sink_row[:, n : n + 1], (rows, 1)) for n in range(heads)], axis=0
            )
            ceiling = jnp.maximum(jnp.max(scores, axis=1, keepdims=True), sink)
            expo = jnp.exp(scores - ceiling).astype(jnp.bfloat16)
            mass = jnp.dot(expo, values, preferred_element_type=jnp.float32)
            seen = mass[:, :HD] / (mass[:, HD : HD + 1] + jnp.exp(sink - ceiling))
            seen = jnp.concatenate(
                [seen[n * rows : (n + 1) * rows] for n in range(heads)], axis=1
            ).astype(jnp.bfloat16)
            part = lax.dot_general(
                seen,
                w_ref[:, first + query_cols + 2 * HD : first + shard_cols],
                (((1,), (1,)), ((), ())),
                preferred_element_type=jnp.float32,
            )
            total = part if total is None else total + part
        sum_ref[step] = total.astype(jnp.bfloat16)

        @pl.when(step < blocks - 1)
        def _():
            out_copy(step, block).start()

        return carry

    lax.fori_loop(0, blocks, one_block, 0)
    own = pltpu.make_async_copy(sum_ref.at[blocks - 1], parts.at[y], own_sem.at[6])
    own.start()
    for step in range(blocks - 1):
        out_copy(step, (y + 3 - step) % 4).wait()
    own.wait()
    edge.wait_send()
    cache_there.wait()
    cache_here.wait()


def attention_layer(tokens, seg_ids, norm_gain, query_weight, kv_weight, out_weight, sinks):
    rows, width = tokens.shape
    col_count = lax.axis_size("col")
    share = query_weight.shape[0]
    padded_share = -(-share // 8) * 8
    extra = padded_share - share
    padded = padded_share * col_count
    xt = jnp.pad(tokens.T.reshape(col_count, share, rows), ((0, 0), (0, extra), (0, 0)))
    xt = xt.reshape(padded, rows)
    gain = jnp.pad(norm_gain.reshape(col_count, share), ((0, 0), (0, extra))).reshape(1, padded)
    shard = jnp.concatenate([query_weight, kv_weight, out_weight.T], axis=1)
    rest, sink_terms = sinks, []
    for _ in range(3):
        term = lax.reduce_precision(rest, 8, 7)
        sink_terms.append(term.astype(jnp.bfloat16))
        rest = rest - term
    sink_terms = jnp.pad(
        jnp.stack(sink_terms), ((0, extra - 3), (0, shard.shape[1] - sinks.shape[0]))
    )
    shard = jnp.concatenate([shard, sink_terms], axis=0)
    seg = jnp.broadcast_to(seg_ids[None, :], (8, rows))
    frequency = jnp.exp(
        (jnp.arange(128, dtype=jnp.int32) % (HD // 2)).astype(jnp.float32)
        * (-2.0 * math.log(theta_base) / HD)
    ).reshape(1, 128)
    vmem = pl.BlockSpec(memory_space=pltpu.VMEM)
    hbm = pl.BlockSpec(memory_space=pl.ANY)
    bf16, f32 = jnp.bfloat16, jnp.float32
    run_rows = 4 * rows
    table = jax.ShapeDtypeStruct((run_rows, 128), f32)
    shard_cols = shard.shape[1]
    x_all, w_all, cosine, sine, position = pl.pallas_call(
        functools.partial(gather_kernel, width),
        out_shape=(
            jax.ShapeDtypeStruct((4, rows, padded), bf16),
            jax.ShapeDtypeStruct((col_count, padded_share, 2 * shard_cols), bf16),
            table,
            table,
            table,
        ),
        in_specs=[vmem, vmem, hbm, vmem, hbm],
        out_specs=(hbm, hbm, vmem, vmem, vmem),
        scratch_shapes=[
            pltpu.VMEM((rows, padded), bf16),
            pltpu.VMEM((5, 4, 8, rows), jnp.int32),
            pltpu.SemaphoreType.DMA((60,)),
            pltpu.SemaphoreType.DMA((60,)),
            pltpu.SemaphoreType.DMA((3,)),
        ],
        compiler_params=pltpu.CompilerParams(
            collective_id=3, has_side_effects=True, vmem_limit_bytes=40 * 2**20
        ),
        name="gather_front",
    )(xt, gain, seg, frequency, shard)
    parts, kv_cache = pl.pallas_call(
        attention_kernel,
        out_shape=(
            jax.ShapeDtypeStruct((4, rows, padded), bf16),
            jax.ShapeDtypeStruct((2 * run_rows, 2 * HD), bf16),
        ),
        in_specs=[hbm, hbm, vmem, vmem, vmem],
        out_specs=(hbm, hbm),
        scratch_shapes=[
            pltpu.VMEM((4, rows, padded), bf16),
            pltpu.VMEM((padded, 2 * shard_cols), bf16),
            pltpu.VMEM((run_rows, 16 * HD), bf16),
            pltpu.VMEM((2, 5 * rows, 2 * HD), bf16),
            pltpu.VMEM((4, rows, padded), bf16),
            pltpu.SemaphoreType.DMA((6,)),
            pltpu.SemaphoreType.DMA((6,)),
            pltpu.SemaphoreType.DMA((7,)),
        ],
        compiler_params=pltpu.CompilerParams(
            collective_id=4, has_side_effects=True, vmem_limit_bytes=58 * 2**20
        ),
        name="attention",
    )(x_all, w_all.reshape(padded, 2 * shard_cols), cosine, sine, position)
    return parts, kv_cache, xt


def slot_grid(routes_t, tokens_here):
    expert_ids = lax.broadcasted_iota(jnp.int32, (EXPERTS, tokens_here), 0)
    hit = jnp.zeros((EXPERTS, tokens_here), jnp.float32)
    for j in range(TOP):
        hit = hit + (routes_t[j : j + 1, :] == expert_ids).astype(jnp.float32)
    earlier = (
        lax.broadcasted_iota(jnp.int32, (tokens_here, tokens_here), 0)
        < lax.broadcasted_iota(jnp.int32, (tokens_here, tokens_here), 1)
    ).astype(jnp.bfloat16)
    rank = jnp.dot(hit.astype(jnp.bfloat16), earlier, preferred_element_type=jnp.float32)
    return hit, rank


def by_slot(hit, rank, amount):
    tokens_here = hit.shape[1]
    slot_ids = lax.broadcasted_iota(jnp.int32, (EXPERTS, 8, tokens_here), 1).astype(jnp.float32)
    first = jnp.where(
        (hit[:, None, :] > 0.5) & (rank[:, None, :] == slot_ids), amount[:, None, :], 0.0
    ).reshape(EXPERTS * 8, tokens_here)
    last = jnp.where((hit > 0.5) & (rank == 8.0), amount, 0.0)
    return first, last


def tiles_of(width):
    return [(k, k * 128, min(128, width - k * 128)) for k in range(-(-width // 128))]


def widen(tile):
    short = 128 - tile.shape[1]
    if short:
        tile = jnp.concatenate([tile, jnp.zeros((tile.shape[0], short), tile.dtype)], axis=1)
    return tile


def pack_message(out_ref, last_ref, tile_first, tile_last, k):
    out_ref[:, k] = widen(tile_first).reshape(EXPERTS, 8, 128).astype(jnp.bfloat16)
    last_ref[pl.ds(k, EXPERTS, stride=24), :] = widen(tile_last)


def finish_message(out_ref, last_ref, tile_count):
    for k in range(tile_count, 24):
        last_ref[pl.ds(k, EXPERTS, stride=24), :] = jnp.zeros((EXPERTS, 128), jnp.float32)
    out_ref[:, tile_count:] = (
        last_ref[...].reshape(EXPERTS, 3, 8, 128).astype(jnp.bfloat16)
    )


def unpack_last(in_ref, last_ref, tile_count):
    last_ref[...] = in_ref[:, tile_count:].astype(jnp.float32).reshape(EXPERTS * 24, 128)


def unpack_tile(in_ref, last_ref, k):
    first = in_ref[:, k].astype(jnp.float32).reshape(EXPERTS * 8, 128)
    last = last_ref[pl.ds(k, EXPERTS, stride=24), :]
    return jnp.concatenate([first, last], axis=0).astype(jnp.bfloat16)


def dispatch_kernel(share, xt_ref, parts_ref, gain_ref, routes_ref, out_ref, hidden_ref, last_ref):
    total = xt_ref[...].astype(jnp.float32).T
    for part in range(parts_ref.shape[0]):
        total = total + parts_ref[part].astype(jnp.float32)
    padded_share = -(-share // 8) * 8
    hidden = jnp.concatenate(
        [total[:, i : i + share] for i in range(0, total.shape[1], padded_share)], axis=1
    )
    hidden_ref[...] = hidden
    moe_in = rms_scale(hidden, gain_ref[...], hidden.shape[1]).astype(jnp.bfloat16)
    hit, rank = slot_grid(routes_ref[...], hidden.shape[0])
    first, last = by_slot(hit, rank, jnp.ones_like(hit))
    first, last = first.astype(jnp.bfloat16), last.astype(jnp.bfloat16)
    tiles = tiles_of(hidden.shape[1])
    for k, start, width in tiles:
        piece = moe_in[:, start : start + width]
        pack_message(
            out_ref,
            last_ref,
            jnp.dot(first, piece, preferred_element_type=jnp.float32),
            jnp.dot(last, piece, preferred_element_type=jnp.float32),
            k,
        )
    finish_message(out_ref, last_ref, len(tiles))


def combine_kernel(hidden_ref, routes_ref, weights_ref, in_ref, out_ref, last_ref):
    routes_t, weights_t = routes_ref[...], weights_ref[...]
    tokens_here = routes_t.shape[1]
    hit, rank = slot_grid(routes_t, tokens_here)
    expert_ids = lax.broadcasted_iota(jnp.int32, (EXPERTS, tokens_here), 0)
    amount = jnp.zeros((EXPERTS, tokens_here), jnp.float32)
    for j in range(TOP):
        amount = amount + jnp.where(
            routes_t[j : j + 1, :] == expert_ids, weights_t[j : j + 1, :], 0.0
        )
    mix = jnp.concatenate(by_slot(hit, rank, amount), axis=0).T
    mix_high = mix.astype(jnp.bfloat16)
    mix_low = (mix - mix_high.astype(jnp.float32)).astype(jnp.bfloat16)
    tiles = tiles_of(out_ref.shape[0])
    unpack_last(in_ref, last_ref, len(tiles))
    for k, start, width in tiles:
        rows = unpack_tile(in_ref, last_ref, k)
        total = jnp.dot(mix_high, rows, preferred_element_type=jnp.float32) + jnp.dot(
            mix_low, rows, preferred_element_type=jnp.float32
        )
        here = slice(start, start + width)
        total = (widen(hidden_ref[:, here]) + total).T
        out_ref[here, :] = total[:width].astype(jnp.bfloat16)


def expert_kernel(
    in_ref, gate_a, up_a, down_a, gate_b, up_b, down_b, out_ref, rows_ref, total_ref, last_ref
):
    half, step = pl.program_id(0), pl.program_id(1)
    width = total_ref.shape[1]
    tiles = tiles_of(width)

    @pl.when((half == 0) & (step == 0))
    def _():
        unpack_last(in_ref, last_ref, len(tiles))
        for k, start, wide in tiles:
            rows_ref[:, start : start + wide] = unpack_tile(in_ref, last_ref, k)[:, :wide]

    def run(gate, up, down, fresh):
        rows = rows_ref[...]
        gate_part = jnp.dot(rows, gate[0], preferred_element_type=jnp.float32)
        up_part = jnp.dot(rows, up[0], preferred_element_type=jnp.float32)
        act = (gate_part * jax.nn.sigmoid(glu_alpha * gate_part) * (up_part + 1.0)).astype(
            jnp.bfloat16
        )
        part = lax.dot_general(
            act, down[0], (((1,), (1,)), ((), ())), preferred_element_type=jnp.float32
        )
        if fresh:
            total_ref[...] = part
        else:
            total_ref[...] += part

    @pl.when((half == 0) & (step == 0))
    def _():
        run(gate_a, up_a, down_a, True)

    @pl.when((half == 0) & (step != 0))
    def _():
        run(gate_a, up_a, down_a, False)

    @pl.when(half == 1)
    def _():
        run(gate_b, up_b, down_b, False)

    @pl.when((half == 1) & (step == pl.num_programs(1) - 1))
    def _():
        for k, start, wide in tiles:
            tile = total_ref[:, start : start + wide]
            pack_message(out_ref, last_ref, tile[: EXPERTS * 8], tile[EXPERTS * 8 :], k)
        finish_message(out_ref, last_ref, len(tiles))


def run_experts(arrived, own_in, own_out, peer_in, peer_out):
    width, half_width = own_in.shape[1], own_out.shape[2]
    chunk = 256
    steps = half_width // chunk
    first = lambda h, s: jnp.where(h == 0, s, steps - 1)
    second = lambda h, s: jnp.where(h == 0, 0, s)
    block_in, block_out = (1, width, chunk), (1, width, chunk)
    specs = []
    for pick in (first, second):
        specs += [
            pl.BlockSpec(block_in, lambda h, s, pick=pick: (0, 0, pick(h, s))),
            pl.BlockSpec(block_in, lambda h, s, pick=pick: (0, 0, pick(h, s) + steps)),
            pl.BlockSpec(block_out, lambda h, s, pick=pick: (0, 0, pick(h, s))),
        ]
    rows = EXPERTS * CAP
    return pl.pallas_call(
        expert_kernel,
        grid=(2, steps),
        out_shape=jax.ShapeDtypeStruct(arrived.shape, arrived.dtype),
        in_specs=[pl.BlockSpec(memory_space=pltpu.VMEM)] + specs,
        out_specs=pl.BlockSpec(memory_space=pltpu.VMEM),
        scratch_shapes=[
            pltpu.VMEM((rows, width), jnp.bfloat16),
            pltpu.VMEM((rows, width), jnp.float32),
            pltpu.VMEM((EXPERTS * 24, 128), jnp.float32),
        ],
        compiler_params=pltpu.CompilerParams(vmem_limit_bytes=60 * 2**20),
        name="experts",
    )(arrived, own_in, own_in, own_out, peer_in, peer_in, peer_out)


def expert_layer(share, xt, parts, moe_gain, routes, route_weights, own, peer):
    tokens_here = routes.shape[0]
    width = moe_gain.shape[0]
    vmem = pl.BlockSpec(memory_space=pltpu.VMEM)
    message = jax.ShapeDtypeStruct((EXPERTS, -(-width // 128) + 3, 8, 128), jnp.bfloat16)
    last = pltpu.VMEM((EXPERTS * 24, 128), jnp.float32)
    outgoing, hidden = pl.pallas_call(
        functools.partial(dispatch_kernel, share),
        out_shape=(message, jax.ShapeDtypeStruct((tokens_here, width), jnp.float32)),
        in_specs=[vmem] * 4,
        out_specs=(vmem, vmem),
        scratch_shapes=[last],
        compiler_params=pltpu.CompilerParams(vmem_limit_bytes=40 * 2**20),
        name="dispatch",
    )(xt, parts, moe_gain.reshape(1, width), routes.T)
    arrived = exchange(outgoing, 1, "exchange_out")
    produced = run_experts(arrived, *own, *peer)
    returned = exchange(produced, 2, "exchange_back")
    mixed = pl.pallas_call(
        combine_kernel,
        out_shape=jax.ShapeDtypeStruct((width, tokens_here), jnp.bfloat16),
        in_specs=[vmem] * 4,
        out_specs=vmem,
        scratch_shapes=[last],
        compiler_params=pltpu.CompilerParams(vmem_limit_bytes=40 * 2**20),
        name="combine",
    )(hidden, routes.T, route_weights.T, returned)
    return mixed.T


def shards(
    tokens,
    seg_ids,
    norm_gain,
    query_weight,
    kv_weight,
    out_weight,
    sinks,
    moe_gain,
    routes,
    route_weights,
    expert_in,
    expert_out,
):
    swap = [(c, c + 1 - 2 * (c % 2)) for c in range(lax.axis_size("col"))]
    own_in, own_out = expert_in, jnp.swapaxes(expert_out, 1, 2)
    peer_in, peer_out = (lax.ppermute(w, "col", swap) for w in (own_in, own_out))
    parts, kv_cache, xt = attention_layer(
        tokens, seg_ids, norm_gain, query_weight, kv_weight, out_weight, sinks
    )
    mixed = expert_layer(
        query_weight.shape[0],
        xt,
        parts,
        moe_gain,
        routes,
        route_weights,
        (own_in, own_out),
        (peer_in, peer_out),
    )
    return (mixed, kv_cache)


def solution(mesh):
    in_specs = (
        P(("col", "row"), None),
        P(("col", "row")),
        P(),
        P("col", "row"),
        P("col", "row"),
        P("row", "col"),
        P("row"),
        P(),
        P(("col", "row"), None),
        P(("col", "row"), None),
        P(("row", "col"), None, None),
        P(("row", "col"), None, None),
    )
    out_specs = (P(("col", "row"), None), P("col", "row"))
    return jax.shard_map(shards, mesh=mesh, in_specs=in_specs, out_specs=out_specs, check_vma=False)
```

time: 492 us -> 255 us (0.52); the launches traced: 483 us -> 254 us
  blocking collectives: 140 us -> 0 us
  Pallas kernels: 138 us -> 238 us
  waiting for transfers between devices: 94.3 us -> 0.01 us
  matrix products: 25.2 us -> 0 us
  local copies, waits for them, and re-layouts: 37.5 us -> 13 us
  loops' own time: 14.7 us -> 0 us
  between operations: 14.7 us -> 0.81 us
  other arithmetic: 14.6 us -> 1.77 us
    all_gather x2 -> x0, blocking collectives: 126 us -> none  [the longest x1 103 us: shards(): lax.all_gather(kv_weight, 'col', axis=0, tiled=True)]
    pallas_call x2 -> x4, Pallas kernels: 3.99 us -> 110 us  [the longest x1 57.1 us: attention_layer(): pl.pallas_call(attention_kernel, out_shape=(jax.ShapeDtypeStruct((4, rows...]
    reduce_scatter x1 -> x0, waiting for transfers between devices: 91.8 us -> none  [shards(): lax.psum_scatter(partial_value.astype(jnp.bfloat16), 'row', scatter_dimen...]
    dot_general x7 -> x0, matrix products: 25.2 us -> none  [the longest x1 7.96 us: shards(): jnp.dot(attended, lax.all_gather(out_weight, 'col', axis=1, tiled=True),...]
    another operation x2 -> x0, loops' own time: 14.7 us -> none  [the longest x1 9.42 us: entering(): return lax.fori_loop(0, place, one, state)]
    unnamed x1 -> x0, blocking collectives: 13.7 us -> none
    unnamed x35 -> x23, local copies, waits for them, and re-layouts: 20.4 us -> 10.1 us
    convert_element_type x1 -> x0, local copies, waits for them, and re-layouts: 8.48 us -> none  [shards(): partial_value.astype(jnp.bfloat16)]
  transfers between devices with their start and end apart: 8 -> 2, of which waited for: 2 -> 0; matrix products, arithmetic and copies ran while one was open for 5% -> 2% of each run, Pallas kernels for 10% -> 63%
where the time goes in v2:
time: 255 us; the launch traced here: 254 us
  Pallas kernels  238 us (93%)
  local copies, waits for them, and re-layouts  13 us (5%)
    pallas_call x2, Pallas kernels, exchange(): pl.pallas_call(exchange_kernel, out_shape=jax.ShapeDtypeStruct(messages.s...  102 us
    pallas_call x1, Pallas kernels, attention_layer(): pl.pallas_call(attention_kernel, out_shape=(jax.ShapeDtypeStruct((4, rows...  57.1 us
    pallas_call x1, Pallas kernels, attention_layer(): pl.pallas_call(functools.partial(gather_kernel, width), out_shape=(jax.Sh...  47.4 us
    pallas_call x1, Pallas kernels, run_experts(): pl.pallas_call(expert_kernel, grid=(2, steps), out_shape=jax.ShapeDtypeSt...  25.8 us
    unnamed x23, local copies, waits for them, and re-layouts  10.1 us
  transfers between devices with their start and end apart: 2, of which 0 were waited for; matrix products, arithmetic and copies ran while one was open for 2% of the time, Pallas kernels for 63%

profile of v2, /device:TPU:2, one launch (start us, length us, event | category | flops | bytes accessed | tf_op | source)
XLA Modules:
  0.0 254.3 jit_solution(13448010259587322437)
XLA Ops:
  0.6 0.0 copy-start.10
  0.6 0.1 collective-permute-start
  0.7 0.5 collective-permute-start.1
  1.2 1.2 reshape.55
  2.5 0.8 reshape.57
  3.3 0.1 reshape.58.gain_ref
  3.4 0.7 reshape.60.gain_ref
  4.1 0.1 pad.12
  4.2 0.7 fusion.9
  4.9 1.1 pad_maximum_fusion.shard_ref
  6.0 0.0 copy-done.10
  6.0 47.4 %gather_front.1 = (bf16[4,128,2944]{2,1,0:T(8,128)(2,1)S(1)}, bf16[16,184,2304]{2,1,0:T(8,128)(2,1)}, f32[512,128]{1,0:T(8,128)S(1)}, f32[512,128]{1,0:T(8,128)S(1)}, f32[512,128]{1,0:T(8,128)S(1)}) custom-call(bf16[2944,128]{1,0:T(8,128)(2,1)S(1)} %bitcast.14, f32[1,2944]{1,0:T(1,128)S(1)} %reshape.58.gain_ref, s32[8,128]{1,0:T(8,128)S(1)} %broadcast_in_dim.2.seg_ref, ...), custom_call_target="tpu_custom_call" | custom-call | tf_op jit(solution)/shard_map/gather_front/pallas_call | solution.py:542
  53.4 0.0 copy-start.3
  53.4 1.7 copy-done.3
  55.0 0.0 copy-start.4
  55.0 0.7 copy-done.4
  55.8 0.0 copy-start.5
  55.8 0.7 copy-done.5
  56.5 0.0 copy-start.6
  56.5 0.7 copy-done.6
  57.2 0.0 copy-start.7
  57.2 57.1 %attention.1 = (bf16[4,128,2944]{2,1,0:T(8,128)(2,1)}, bf16[1024,128]{1,0:T(8,128)(2,1)}) custom-call(bf16[4,128,2944]{2,1,0:T(8,128)(2,1)} %copy-done.3, bf16[2944,2304]{1,0:T(8,128)(2,1)} %bitcast.19, f32[512,128]{1,0:T(8,128)} %copy-done.4, f32[512,128]{1,0:T(8,128)} %copy-done.5, f32[512,128]{1,0:T(8,128)} %copy-done.6), custom_call_target="tpu_custom_call" | custom-call | tf_op jit(solution)/shard_map/attention/pallas_call | solution.py:565
  114.3 0.0 copy-done.7
  114.3 0.0 copy-start.2
  114.3 1.8 copy-done.2
  116.2 2.3 dispatch.1
  118.4 0.0 copy-start.1
  118.4 1.7 copy-done.1
  120.2 53.3 %exchange_out.1.in_ref = bf16[64,26,8,128]{3,2,1,0:T(8,128)(2,1)} custom-call(bf16[64,26,8,128]{3,2,1,0:T(8,128)(2,1)} %copy-done.1), custom_call_target="tpu_custom_call" | custom-call | tf_op jit(solution)/shard_map/exchange_out/pallas_call | solution.py:84
  173.5 0.0 collective-permute-done.1.down_b
  173.5 0.0 collective-permute-done.gate_b.up_b
  173.5 25.8 %experts.1.out_msgs = bf16[64,26,8,128]{3,2,1,0:T(8,128)(2,1)} custom-call(bf16[64,26,8,128]{3,2,1,0:T(8,128)(2,1)} %exchange_out.1.in_ref, bf16[1,2880,1536]{2,1,0:T(8,128)(2,1)} %up_a.1, bf16[1,2880,1536]{2,1,0:T(8,128)(2,1)} %up_a.1, bf16[1,2880,768]{2,1,0:T(8,128)(2,1)} %bitcast.21, bf16[1,2880,1536]{2,1,0:T(8,128)(2,1)} %collective-permute-done.gate_b.up_b, ...), custom_call_target="tpu_custom_call" | custom-call | tf_op jit(solution)/shard_map/experts/pallas_call | solution.py:762
  199.3 0.0 copy-start.8
  199.3 0.0 copy-start.9
  199.3 48.9 %exchange_back.1.in_ref = bf16[64,26,8,128]{3,2,1,0:T(8,128)(2,1)} custom-call(bf16[64,26,8,128]{3,2,1,0:T(8,128)(2,1)} %experts.1.out_msgs), custom_call_target="tpu_custom_call" | custom-call | tf_op jit(solution)/shard_map/exchange_back/pallas_call | solution.py:84
  248.2 0.0 copy-done.8
  248.2 0.0 copy-start
  248.2 2.0 copy-done
  250.2 3.4 %combine.1 = bf16[2880,128]{1,0:T(8,128)(2,1)} custom-call(f32[128,2880]{1,0:T(8,128)S(1)} %get-tuple-element.17.hidden_ref, s32[4,128]{1,0:T(4,128)S(1)} %bitcast.17, f32[4,128]{1,0:T(4,128)S(1)} %bitcast.18, bf16[64,26,8,128]{3,2,1,0:T(8,128)(2,1)S(1)} %copy-done), custom_call_target="tpu_custom_call" | custom-call | tf_op jit(solution)/shard_map/combine/pallas_call | solution.py:796
  253.6 0.0 copy-done.9
  253.6 0.7 copy.15
  (4 shorter events, 0.0 us)
Async XLA Ops:
  0.6 5.3 %copy-start.10 = (s32[128]{0:T(128)S(1)}, s32[128]{0:T(128)}, u32[]{:S(2)}) copy-start(s32[128]{0:T(128)} %param.13) | copy-start | bytes 1540
  0.6 172.9 %collective-permute-start = (bf16[1,2880,1536]{2,1,0:T(8,128)(2,1)}, bf16[1,2880,1536]{2,1,0:T(8,128)(2,1)}, u32[]{:S(2)}, u32[]{:S(2)}) collective-permute-start(bf16[1,2880,1536]{2,1,0:T(8,128)(2,1)} %up_a.1), channel_id=1, source_target_pairs={{0,1},{1,0},{2,3},{3,2},{4,5},{5,4},{6,7},{7,6},{8,9},{9,8},{10,11... | collective-permute-start | bytes 26542088 | tf_op jit(solution)/shard_map/ppermute | solution.py:824
  0.7 172.7 %collective-permute-start.1 = (bf16[1,2880,768]{2,1,0:T(8,128)(2,1)}, bf16[1,2880,768]{2,1,0:T(8,128)(2,1)}, u32[]{:S(2)}, u32[]{:S(2)}) collective-permute-start(bf16[1,2880,768]{2,1,0:T(8,128)(2,1)} %bitcast.20), channel_id=1, source_target_pairs={{0,1},{1,0},{2,3},{3,2},{4,5},{5,4},{6,7},{7,6},{8,9},{9,8},{10,11... | collective-permute-start | bytes 13271048 | tf_op jit(solution)/shard_map/ppermute | solution.py:824
  53.4 1.7 copy-start.3
  55.0 0.7 copy-start.4
  55.8 0.7 copy-start.5
  56.5 0.7 copy-start.6
  57.2 57.1 %copy-start.7 = (s32[128,4]{0,1:T(4,128)S(1)}, s32[128,4]{0,1:T(4,128)}, u32[]{:S(2)}) copy-start(s32[128,4]{0,1:T(4,128)} %param.20) | copy-start | bytes 6148
  114.3 1.9 copy-start.2
  118.4 1.8 copy-start.1
  199.3 49.0 %copy-start.8 = (f32[128,4]{0,1:T(4,128)S(1)}, f32[128,4]{0,1:T(4,128)}, u32[]{:S(2)}) copy-start(f32[128,4]{0,1:T(4,128)} %param.21) | copy-start | bytes 6148
  199.3 54.3 %copy-start.9 = (bf16[1024,128]{1,0:T(8,128)(2,1)S(1)}, bf16[1024,128]{1,0:T(8,128)(2,1)}, u32[]{:S(2)}) copy-start(bf16[1024,128]{1,0:T(8,128)(2,1)} %get-tuple-element.26) | copy-start | bytes 786436
  248.2 2.0 copy-start

commit v3 on v2

v3 whole, which is shorter than its diff:
```python
import functools
import math

import jax
import jax.numpy as jnp
import numpy as np
from jax import lax
from jax.experimental import pallas as pl
from jax.experimental.pallas import tpu as pltpu
from jax.sharding import PartitionSpec as P

HD = 64
WIN = 128
EXPERTS = 64
TOP = 4
CAP = 9
SEGS = 16


eps_norm = 1e-05
theta_base = 150000.0
glu_alpha = 1.702
masked_score = -1e30


def rms_scale(widened, gain_vec, width):
    mean_square = jnp.sum(widened * widened, axis=-1, keepdims=True) * (1.0 / width)
    return widened * lax.rsqrt(mean_square + eps_norm) * gain_vec


def chip_place():
    row, col = lax.axis_index("row"), lax.axis_index("col")
    return (row // 4) * 2 + (col // 2) % 2, row % 4, col // 4, col % 2


def device_at(x, y, z, core):
    return ((x // 2) * 4 + y, z * 4 + (x % 2) * 2 + core)


def expert_at(x, y, z):
    return ((x // 2) * 4 + y) * 8 + z * 2 + x % 2


def hop_order():
    every = [
        (dx, (t + dx) % 4, (t // 4 + dx) % 4) for t in range(16) for dx in (1, 3, 2, 0)
    ]
    return [v for v in every if v != (0, 0, 0)]


def exchange_kernel(out_msgs, in_msgs, send_sem, recv_sem, own_sem):
    x, y, z, core = chip_place()
    me = expert_at(x, y, z)
    offsets = hop_order()
    barrier = pltpu.get_barrier_semaphore()
    for dx, dy, dz in offsets:
        pl.semaphore_signal(
            barrier,
            inc=1,
            device_id=device_at((x + dx) % 4, (y + dy) % 4, (z + dz) % 4, core),
            device_id_type=pl.DeviceIdType.MESH,
        )
    own = pltpu.make_async_copy(out_msgs.at[me], in_msgs.at[me], own_sem)
    own.start()
    pl.semaphore_wait(barrier, len(offsets))
    copies = []
    for number, (dx, dy, dz) in enumerate(offsets):
        there = ((x + dx) % 4, (y + dy) % 4, (z + dz) % 4)
        copy = pltpu.make_async_remote_copy(
            src_ref=out_msgs.at[expert_at(*there)],
            dst_ref=in_msgs.at[me],
            send_sem=send_sem.at[number],
            recv_sem=recv_sem.at[number],
            device_id=device_at(*there, core),
            device_id_type=pl.DeviceIdType.MESH,
        )
        copy.start()
        copies.append(copy)
    own.wait()
    for copy in copies:
        copy.wait()


def exchange(messages, ident, name):
    others = EXPERTS - 1
    return pl.pallas_call(
        exchange_kernel,
        out_shape=jax.ShapeDtypeStruct(messages.shape, messages.dtype),
        in_specs=[pl.BlockSpec(memory_space=pl.ANY)],
        out_specs=pl.BlockSpec(memory_space=pl.ANY),
        scratch_shapes=[
            pltpu.SemaphoreType.DMA((others,)),
            pltpu.SemaphoreType.DMA((others,)),
            pltpu.SemaphoreType.DMA,
        ],
        compiler_params=pltpu.CompilerParams(collective_id=ident, has_side_effects=True),
        name=name,
    )(messages)


def described(source, target, sems, number, device):
    return pltpu.make_async_remote_copy(
        src_ref=source,
        dst_ref=target,
        send_sem=sems[0].at[number],
        recv_sem=sems[1].at[number],
        device_id=device,
        device_id_type=pl.DeviceIdType.MESH,
    )


def send(*parts):
    copy = described(*parts)
    copy.start()
    return copy


def greet(devices):
    barrier = pltpu.get_barrier_semaphore()
    for device in devices:
        pl.semaphore_signal(
            barrier, inc=1, device_id=device, device_id_type=pl.DeviceIdType.MESH
        )
    pl.semaphore_wait(barrier, len(devices))


class Ring:
    def __init__(self, own, place, device, sems, first):
        self.place, self.device, self.sems, self.first = place, device, sems, first
        self.sent = [
            self.pass_on(0, own(0), 0, 0, 1),
            self.pass_on(1, own(1), 0, 1, 1),
            self.pass_on(2, own(1), 0, 1, 3),
            self.pass_on(3, own(0), 0, 0, 3),
        ]

    def pass_on(self, number, source, owner, half, to):
        return send(
            source, self.place(owner, half), self.sems, self.first + number, self.device(to)
        )

    def take_left(self):
        self.sent[0].wait_recv()
        self.sent.append(self.pass_on(4, self.place(3, 0), 3, 0, 1))
        self.sent[1].wait_recv()

    def take_right(self):
        self.sent[2].wait_recv()
        self.sent.append(self.pass_on(5, self.place(1, 1), 1, 1, 3))
        self.sent[3].wait_recv()

    def take_far(self):
        self.sent[4].wait_recv()
        self.sent[5].wait_recv()

    def close(self):
        for copy in self.sent:
            copy.wait_send()


SHARD_CUT = 96
QUERY_LANES = 8 * HD
PROJ_LANES = QUERY_LANES + 2 * HD


def front_kernel(
    width,
    share,
    xt_ref,
    gain_ref,
    seg_ref,
    freq_ref,
    shard_ref,
    routes_ref,
    out_ref,
    hidden_ref,
    kv_out,
    x_ref,
    w_ref,
    window_ref,
    cos_ref,
    sin_ref,
    pos_ref,
    query_ref,
    kv_ref,
    sum_ref,
    far_ref,
    parts_ref,
    last_ref,
    send_sem,
    recv_sem,
    own_sem,
):
    x, y, z, core = chip_place()
    sems = (send_sem, recv_sem)
    side = x // 2
    run = lax.axis_index("col") * 2 + side
    runs = 2 * lax.axis_size("col")
    shard_rows = shard_ref.shape[0]
    blocks, rows, padded = x_ref.shape
    every = blocks * rows

    def at(first, second):
        return (
            (x + first * core + second * (1 - core)) % 4,
            (z + first * (1 - core) + second * core) % 4,
        )

    def chip(first, second):
        there_x, there_z = at(first, second)
        return device_at(there_x, y, there_z, core)

    def run_device(steps):
        there = (run + steps + runs) % runs
        return ((there % 2) * 4 + y, there // 2)

    def y_device(steps):
        return device_at(x, (y + steps) % 4, z, core)

    sister = device_at(x, y, z, 1 - core)
    partner = device_at((x + 2) % 4, y, z, core)
    greet(
        [y_device(s) for s in (1, 2, 3)]
        + [chip(s, 0) for s in (1, 3)]
        + [chip(0, s) for s in (1, 3)]
        + [sister, partner]
        + [run_device(s) for s in (1, 2, 3, 4, -1, -2, -3, -4)]
    )
    own_seg = pltpu.make_async_copy(seg_ref, window_ref.at[0, y], own_sem.at[0])
    own_seg.start()
    seg_sent = [
        send(seg_ref, window_ref.at[0, y], sems, n, y_device(s)) for n, s in enumerate((1, 2, 3))
    ]

    class Stream:
        def __init__(self, first_sem):
            self.first_sem = first_sem
            self.to_sister, self.rings = [], {}
            self.own = pltpu.make_async_copy(
                self.shard(pl.ds(0, shard_rows)),
                self.place(0, 0, pl.ds(0, shard_rows)),
                own_sem.at[1],
            )
            self.own.start()
            self.along = Ring(
                self.own_half,
                lambda o, h: self.half(o, 0, h),
                lambda s: chip(s, 0),
                sems,
                first_sem,
            )
            self.across(0)

        def shard(self, rows_here):
            return shard_ref.at[rows_here]

        def place(self, first, second, rows_here):
            there_x, there_z = at(first, second)
            slot = there_z * 4 + (there_x % 2) * 2 + core
            start = pl.multiple_of(slot * shard_rows + rows_here.start, 16)
            return w_ref.at[there_x // 2, pl.ds(start, rows_here.size)]

        def cut(self, half):
            if half == 0:
                return pl.ds(0, SHARD_CUT)
            return pl.ds(SHARD_CUT, shard_rows - SHARD_CUT)

        def own_half(self, half):
            return self.shard(self.cut(half))

        def half(self, first, second, half):
            return self.place(first, second, self.cut(half))

        def across(self, owner):
            own = self.own_half if owner == 0 else (lambda h: self.half(owner, 0, h))
            self.rings[owner] = Ring(
                own,
                lambda o, h: self.half(owner, o, h),
                lambda s: chip(0, s),
                sems,
                self.first_sem + 6 + 6 * len(self.rings),
            )
            self.hand_over(owner, 0)

        def hand_over(self, first, second):
            place = self.place(first, second, pl.ds(0, shard_rows))
            own = (first, second) == (0, 0)
            source = self.shard(pl.ds(0, shard_rows)) if own else place
            number = self.first_sem + 30 + len(self.to_sister)
            self.to_sister.append(send(source, place, sems, number, sister))

        def near(self, owner):
            self.rings[owner].take_left()
            self.hand_over(owner, 3)
            self.rings[owner].take_right()
            self.hand_over(owner, 1)

        def far(self, owner):
            self.rings[owner].take_far()
            self.hand_over(owner, 2)

        def arrived(self):
            self.own.wait()
            for copy in self.to_sister:
                copy.wait_recv()

        def close(self):
            for ring in [self.along] + list(self.rings.values()):
                ring.close()
            for copy in self.to_sister:
                copy.wait_send()

    proj = Stream(20)

    raw = xt_ref[...].astype(jnp.float32).T
    normed = rms_scale(raw, gain_ref[0:1, :], width)
    gap = jnp.zeros((rows, shard_rows - share), jnp.float32)
    x_ref[y] = jnp.concatenate(
        [piece for i in range(0, width, share) for piece in (normed[:, i : i + share], gap)],
        axis=1,
    ).astype(jnp.bfloat16)

    own_seg.wait()
    for copy in seg_sent:
        copy.wait_recv()
    seg_on = [
        send(window_ref.at[0], window_ref.at[s], sems, 2 + s, run_device(s)) for s in (1, 2, 3, 4)
    ]
    half_rows = rows // 2
    upper, lower = pl.ds(0, half_rows), pl.ds(half_rows, half_rows)
    x_place = lambda o, h: x_ref.at[(y + o) % 4, lower if h else upper]
    tokens_ring = Ring(lambda h: x_place(0, h), x_place, y_device, sems, 7)

    proj.along.take_left()
    proj.across(3)
    proj.along.take_right()
    proj.across(1)
    proj.rings[0].take_left()
    proj.hand_over(0, 3)
    proj.rings[0].take_right()
    proj.hand_over(0, 1)
    tokens_ring.take_left()
    tokens_ring.take_right()
    proj.along.take_far()
    proj.across(2)
    proj.near(3)
    for copy in seg_on:
        copy.wait_recv()
    fill_tables(run, window_ref, freq_ref, cos_ref, sin_ref, pos_ref)
    proj.near(1)
    proj.near(2)
    for owner in (0, 3, 1, 2):
        proj.far(owner)
    tokens_ring.take_far()
    proj.arrived()

    cosine, sine = cos_ref[...], sin_ref[...]
    lane = lax.broadcasted_iota(jnp.int32, cosine.shape, 1)

    edges = []

    def project(h):
        mixed_kv = jnp.dot(
            x_ref[...].reshape(every, padded),
            w_ref[h, :, :PROJ_LANES],
            preferred_element_type=jnp.float32,
        )
        kv = mixed_kv[:, QUERY_LANES:]
        kv = jnp.where(lane < HD, turned(kv, cosine, sine), kv)
        kv_ref[h, pl.ds(rows, every), :] = kv.astype(jnp.bfloat16)
        edges.append(
            send(
                kv_ref.at[h, pl.ds(every, rows)],
                kv_ref.at[h, pl.ds(0, rows)],
                sems,
                66 + h,
                run_device(1),
            )
        )
        for k in range(0, QUERY_LANES, 128):
            tile = turned(mixed_kv[:, k : k + 128], cosine, sine) * HD**-0.5
            query_ref[:, h * QUERY_LANES + k : h * QUERY_LANES + k + 128] = tile.astype(
                jnp.bfloat16
            )

    project(0)
    project(1)
    mine = pl.ds(pl.multiple_of(side * every, every), every)
    cache_there = send(
        kv_ref.at[1 - side, pl.ds(rows, every)], kv_out.at[mine], sems, 14, partner
    )
    cache_here = pltpu.make_async_copy(
        kv_ref.at[side, pl.ds(rows, every)], kv_out.at[mine], own_sem.at[3]
    )
    cache_here.start()
    for edge in edges:
        edge.wait_recv()
    distance = (
        rows
        + lax.broadcasted_iota(jnp.int32, (rows, 2 * rows), 0)
        - lax.broadcasted_iota(jnp.int32, (rows, 2 * rows), 1)
    ).astype(jnp.float32)

    right, left = y_device(1), y_device(3)
    far_a = (sum_ref.at[0, upper], far_ref.at[0], sems, 15, right)
    far_b = (sum_ref.at[0, lower], far_ref.at[1], sems, 16, left)
    right_b = (sum_ref.at[1, lower], parts_ref.at[0, lower], sems, 17, right)
    left_a = (sum_ref.at[2, upper], parts_ref.at[1, upper], sems, 18, left)
    right_a = (sum_ref.at[1, upper], parts_ref.at[0, upper], sems, 19, right)
    left_b = (sum_ref.at[2, lower], parts_ref.at[1, lower], sems, 13, left)

    def one_block(step, carry):
        block = (y + 10 - step + (step // 2) * (7 - 2 * step)) % 4
        here = pl.ds(pl.multiple_of(block * rows, rows), rows)
        sum_ref[step] = block_sum(
            here,
            pl.ds(pl.multiple_of(block * rows, rows), 2 * rows),
            distance,
            pos_ref,
            query_ref,
            kv_ref,
            w_ref,
        ).astype(jnp.bfloat16)

        @pl.when(step == 0)
        def _():
            send(*far_a)
            send(*far_b)

        @pl.when(step == 1)
        def _():
            send(*right_b)

        @pl.when(step == 2)
        def _():
            send(*left_a)

        return carry

    lax.fori_loop(0, blocks, one_block, 0)
    far_a, far_b, right_b, left_a = (described(*c) for c in (far_a, far_b, right_b, left_a))
    far_a.wait_recv()
    sum_ref[1, upper] = (
        sum_ref[1, upper].astype(jnp.float32) + far_ref[0].astype(jnp.float32)
    ).astype(jnp.bfloat16)
    right_a = send(*right_a)
    far_b.wait_recv()
    sum_ref[2, lower] = (
        sum_ref[2, lower].astype(jnp.float32) + far_ref[1].astype(jnp.float32)
    ).astype(jnp.bfloat16)
    left_b = send(*left_b)
    proj.close()
    tokens_ring.close()
    for copy in seg_sent + seg_on + edges + [far_a, far_b]:
        copy.wait_send()
    total = sum_ref[blocks - 1].astype(jnp.float32)
    hit, rank = slot_grid(routes_ref[...], rows)
    first, last = by_slot(hit, rank, jnp.ones_like(hit))
    for copy in (right_b, left_a, right_a, left_b, cache_there, cache_here):
        copy.wait()
    total = total + parts_ref[0].astype(jnp.float32) + parts_ref[1].astype(jnp.float32)
    hidden = jnp.concatenate(
        [total[:, i : i + share] for i in range(0, padded, shard_rows)], axis=1
    )
    hidden = hidden + xt_ref[...].astype(jnp.float32).T
    hidden_ref[...] = hidden
    moe_in = rms_scale(hidden, gain_ref[1:2, :], width).astype(jnp.bfloat16)
    first, last = first.astype(jnp.bfloat16), last.astype(jnp.bfloat16)
    tiles = tiles_of(width)
    for k, start, wide in tiles:
        piece = moe_in[:, start : start + wide]
        pack_message(
            out_ref,
            last_ref,
            jnp.dot(first, piece, preferred_element_type=jnp.float32),
            jnp.dot(last, piece, preferred_element_type=jnp.float32),
            k,
        )
    finish_message(out_ref, last_ref, len(tiles))


def block_sum(here, near, distance, pos_ref, query_ref, kv_ref, w_ref):
    rows = distance.shape[0]
    heads = QUERY_LANES // HD
    position = pos_ref[here, :]
    position = jnp.concatenate([position, position], axis=1)
    allowed = (distance >= 0) & (distance < WIN) & (distance <= position)
    allowed = jnp.concatenate([allowed.astype(jnp.float32)] * heads, axis=0) > 0.5
    total = None
    for h in range(2):
        keys = kv_ref[h, near, :]
        values = jnp.where(
            lax.broadcasted_iota(jnp.int32, keys.shape, 1) < HD,
            pltpu.roll(keys.astype(jnp.float32), HD, 1),
            1.0,
        ).astype(jnp.bfloat16)
        query = query_ref[here, h * QUERY_LANES : (h + 1) * QUERY_LANES]
        query = jnp.concatenate([query[:, n * HD : (n + 1) * HD] for n in range(heads)], axis=0)
        scores = lax.dot_general(
            query,
            keys[:, :HD],
            (((1,), (1,)), ((), ())),
            preferred_element_type=jnp.float32,
        )
        scores = jnp.where(allowed, scores, masked_score)
        sink_rows = w_ref[h, 176:192, 0:128].astype(jnp.float32)
        sink_row = jnp.sum(sink_rows[4:8], axis=0, keepdims=True)
        sink = jnp.concatenate(
            [jnp.broadcast_to(sink_row[:, n : n + 1], (rows, 1)) for n in range(heads)], axis=0
        )
        ceiling = jnp.maximum(jnp.max(scores, axis=1, keepdims=True), sink)
        expo = jnp.exp(scores - ceiling).astype(jnp.bfloat16)
        mass = jnp.dot(expo, values, preferred_element_type=jnp.float32)
        seen = mass[:, :HD] / (mass[:, HD : HD + 1] + jnp.exp(sink - ceiling))
        seen = jnp.concatenate(
            [seen[n * rows : (n + 1) * rows] for n in range(heads)], axis=1
        ).astype(jnp.bfloat16)
        part = lax.dot_general(
            seen,
            w_ref[h, :, PROJ_LANES:],
            (((1,), (1,)), ((), ())),
            preferred_element_type=jnp.float32,
        )
        total = part if total is None else total + part
    return total


def circle(angle):
    quarter = jnp.floor(angle * (2.0 / math.pi) + 0.5)
    rest = angle - quarter * 1.5703125
    rest = rest - quarter * 4.837512969970703125e-4
    rest = rest - quarter * 7.54978995489188216e-8
    square = rest * rest
    low = rest + rest * square * (
        -1.6666654611e-1 + square * (8.3321608736e-3 - square * 1.9515295891e-4)
    )
    high = (1.0 - 0.5 * square) + square * square * (
        4.166664568298827e-2 + square * (-1.388731625493765e-3 + square * 2.443315711809948e-5)
    )
    turn = quarter.astype(jnp.int32) % 4
    odd = turn % 2 == 1
    sine, cosine = jnp.where(odd, high, low), jnp.where(odd, low, high)
    return (
        jnp.where((turn == 1) | (turn == 2), -cosine, cosine),
        jnp.where(turn >= 2, -sine, sine),
    )


def fill_tables(run, window_ref, freq_ref, cos_ref, sin_ref, pos_ref):
    span, parts, _, lanes = window_ref.shape
    ids = [
        jnp.where(run - s >= 0, window_ref[s].reshape(parts * 8, lanes), -1).astype(jnp.float32)
        for s in range(span)
    ]
    ids = jnp.concatenate(ids, axis=0)
    fewer = [
        jnp.sum((ids < float(s)).astype(jnp.float32), keepdims=True) * 0.125 for s in range(SEGS)
    ]
    lane = lax.broadcasted_iota(jnp.int32, (lanes, lanes), 1)
    row = lax.broadcasted_iota(jnp.int32, (lanes, lanes), 0).astype(jnp.float32)
    for part in range(parts):
        own = window_ref[0, part].astype(jnp.float32)
        own = jnp.broadcast_to(own[0:1, :], (lanes, lanes)).T
        start = jnp.zeros((lanes, lanes), jnp.float32)
        for s in range(SEGS):
            start = jnp.where(own == float(s), fewer[s], start)
        position = row + float((span - 1) * parts * lanes + part * lanes) - start
        angle = position * freq_ref[...]
        cosine, sine = circle(angle)
        here = pl.ds(part * lanes, lanes)
        cos_ref[here, :] = cosine
        sin_ref[here, :] = jnp.where(lane % HD < HD // 2, -sine, sine)
        pos_ref[here, :] = position


def turned(tile, cosine, sine):
    lane = lax.broadcasted_iota(jnp.int32, tile.shape, 1)
    other = jnp.where(
        lane % HD < HD // 2, pltpu.roll(tile, 128 - HD // 2, 1), pltpu.roll(tile, HD // 2, 1)
    )
    return tile * cosine + other * sine


def attention_layer(
    tokens, seg_ids, norm_gain, query_weight, kv_weight, out_weight, sinks, moe_gain, routes
):
    rows, width = tokens.shape
    col_count = lax.axis_size("col")
    share = query_weight.shape[0]
    padded_share = -(-share // 16) * 16
    extra = padded_share - share
    padded = padded_share * col_count
    gains = jnp.stack([norm_gain, moe_gain])
    shard = jnp.concatenate([query_weight, kv_weight, out_weight.T], axis=1)
    rest, sink_terms = sinks, []
    for _ in range(3):
        term = lax.reduce_precision(rest, 8, 7)
        sink_terms.append(term.astype(jnp.bfloat16))
        rest = rest - term
    sink_terms = jnp.pad(
        jnp.stack(sink_terms), ((0, extra - 3), (0, shard.shape[1] - sinks.shape[0]))
    )
    shard = jnp.concatenate([shard, sink_terms], axis=0)
    seg = jnp.broadcast_to(seg_ids[None, :], (8, rows))
    frequency = jnp.asarray(
        np.exp((np.arange(128) % (HD // 2)) * (-2.0 * math.log(theta_base) / HD))[None, :],
        jnp.float32,
    )
    vmem = pl.BlockSpec(memory_space=pltpu.VMEM)
    hbm = pl.BlockSpec(memory_space=pl.ANY)
    bf16, f32 = jnp.bfloat16, jnp.float32
    sem = pltpu.SemaphoreType.DMA
    return pl.pallas_call(
        functools.partial(front_kernel, width, share),
        out_shape=(
            jax.ShapeDtypeStruct((EXPERTS, -(-width // 128) + 3, 8, 128), bf16),
            jax.ShapeDtypeStruct((rows, width), f32),
            jax.ShapeDtypeStruct((8 * rows, 2 * HD), bf16),
        ),
        in_specs=[vmem, vmem, hbm, vmem, hbm, vmem],
        out_specs=(vmem, vmem, hbm),
        scratch_shapes=[
            pltpu.VMEM((4, rows, padded), bf16),
            pltpu.VMEM((2, padded, shard.shape[1]), bf16),
            pltpu.VMEM((5, 4, 8, rows), jnp.int32),
            pltpu.VMEM((4 * rows, 128), f32),
            pltpu.VMEM((4 * rows, 128), f32),
            pltpu.VMEM((4 * rows, 128), f32),
            pltpu.VMEM((4 * rows, 2 * QUERY_LANES), bf16),
            pltpu.VMEM((2, 5 * rows, 2 * HD), bf16),
            pltpu.VMEM((4, rows, padded), bf16),
            pltpu.VMEM((2, rows // 2, padded), bf16),
            pltpu.VMEM((2, rows, padded), bf16),
            pltpu.VMEM((EXPERTS * 24, 128), f32),
            sem((68,)),
            sem((68,)),
            sem((4,)),
        ],
        compiler_params=pltpu.CompilerParams(
            collective_id=3, has_side_effects=True, vmem_limit_bytes=58 * 2**20
        ),
        name="front",
    )(tokens.T, gains, seg, frequency, shard, routes.T)


def slot_grid(routes_t, tokens_here):
    expert_ids = lax.broadcasted_iota(jnp.int32, (EXPERTS, tokens_here), 0)
    hit = jnp.zeros((EXPERTS, tokens_here), jnp.float32)
    for j in range(TOP):
        hit = hit + (routes_t[j : j + 1, :] == expert_ids).astype(jnp.float32)
    earlier = (
        lax.broadcasted_iota(jnp.int32, (tokens_here, tokens_here), 0)
        < lax.broadcasted_iota(jnp.int32, (tokens_here, tokens_here), 1)
    ).astype(jnp.bfloat16)
    rank = jnp.dot(hit.astype(jnp.bfloat16), earlier, preferred_element_type=jnp.float32)
    return hit, rank


def by_slot(hit, rank, amount):
    tokens_here = hit.shape[1]
    slot_ids = lax.broadcasted_iota(jnp.int32, (EXPERTS, 8, tokens_here), 1).astype(jnp.float32)
    first = jnp.where(
        (hit[:, None, :] > 0.5) & (rank[:, None, :] == slot_ids), amount[:, None, :], 0.0
    ).reshape(EXPERTS * 8, tokens_here)
    last = jnp.where((hit > 0.5) & (rank == 8.0), amount, 0.0)
    return first, last


def tiles_of(width):
    return [(k, k * 128, min(128, width - k * 128)) for k in range(-(-width // 128))]


def widen(tile):
    short = 128 - tile.shape[1]
    if short:
        tile = jnp.concatenate([tile, jnp.zeros((tile.shape[0], short), tile.dtype)], axis=1)
    return tile


def pack_message(out_ref, last_ref, tile_first, tile_last, k):
    out_ref[:, k] = widen(tile_first).reshape(EXPERTS, 8, 128).astype(jnp.bfloat16)
    last_ref[pl.ds(k, EXPERTS, stride=24), :] = widen(tile_last)


def finish_message(out_ref, last_ref, tile_count):
    for k in range(tile_count, 24):
        last_ref[pl.ds(k, EXPERTS, stride=24), :] = jnp.zeros((EXPERTS, 128), jnp.float32)
    out_ref[:, tile_count:] = (
        last_ref[...].reshape(EXPERTS, 3, 8, 128).astype(jnp.bfloat16)
    )


def unpack_last(in_ref, last_ref, tile_count):
    last_ref[...] = in_ref[:, tile_count:].astype(jnp.float32).reshape(EXPERTS * 24, 128)


def unpack_tile(in_ref, last_ref, k):
    first = in_ref[:, k].astype(jnp.float32).reshape(EXPERTS * 8, 128)
    last = last_ref[pl.ds(k, EXPERTS, stride=24), :]
    return jnp.concatenate([first, last], axis=0).astype(jnp.bfloat16)


def combine_kernel(hidden_ref, routes_ref, weights_ref, in_ref, out_ref, last_ref):
    routes_t, weights_t = routes_ref[...], weights_ref[...]
    tokens_here = routes_t.shape[1]
    hit, rank = slot_grid(routes_t, tokens_here)
    expert_ids = lax.broadcasted_iota(jnp.int32, (EXPERTS, tokens_here), 0)
    amount = jnp.zeros((EXPERTS, tokens_here), jnp.float32)
    for j in range(TOP):
        amount = amount + jnp.where(
            routes_t[j : j + 1, :] == expert_ids, weights_t[j : j + 1, :], 0.0
        )
    mix = jnp.concatenate(by_slot(hit, rank, amount), axis=0).T
    mix_high = mix.astype(jnp.bfloat16)
    mix_low = (mix - mix_high.astype(jnp.float32)).astype(jnp.bfloat16)
    tiles = tiles_of(out_ref.shape[0])
    unpack_last(in_ref, last_ref, len(tiles))
    for k, start, width in tiles:
        rows = unpack_tile(in_ref, last_ref, k)
        total = jnp.dot(mix_high, rows, preferred_element_type=jnp.float32) + jnp.dot(
            mix_low, rows, preferred_element_type=jnp.float32
        )
        here = slice(start, start + width)
        total = (widen(hidden_ref[:, here]) + total).T
        out_ref[here, :] = total[:width].astype(jnp.bfloat16)


def expert_kernel(
    in_ref, gate_a, up_a, down_a, gate_b, up_b, down_b, out_ref, rows_ref, total_ref, last_ref
):
    half, step = pl.program_id(0), pl.program_id(1)
    width = total_ref.shape[1]
    tiles = tiles_of(width)

    @pl.when((half == 0) & (step == 0))
    def _():
        unpack_last(in_ref, last_ref, len(tiles))
        for k, start, wide in tiles:
            rows_ref[:, start : start + wide] = unpack_tile(in_ref, last_ref, k)[:, :wide]

    def run(gate, up, down, fresh):
        rows = rows_ref[...]
        gate_part = jnp.dot(rows, gate[0], preferred_element_type=jnp.float32)
        up_part = jnp.dot(rows, up[0], preferred_element_type=jnp.float32)
        act = (gate_part * jax.nn.sigmoid(glu_alpha * gate_part) * (up_part + 1.0)).astype(
            jnp.bfloat16
        )
        part = lax.dot_general(
            act, down[0], (((1,), (1,)), ((), ())), preferred_element_type=jnp.float32
        )
        if fresh:
            total_ref[...] = part
        else:
            total_ref[...] += part

    @pl.when((half == 0) & (step == 0))
    def _():
        run(gate_a, up_a, down_a, True)

    @pl.when((half == 0) & (step != 0))
    def _():
        run(gate_a, up_a, down_a, False)

    @pl.when(half == 1)
    def _():
        run(gate_b, up_b, down_b, False)

    @pl.when((half == 1) & (step == pl.num_programs(1) - 1))
    def _():
        for k, start, wide in tiles:
            tile = total_ref[:, start : start + wide]
            pack_message(out_ref, last_ref, tile[: EXPERTS * 8], tile[EXPERTS * 8 :], k)
        finish_message(out_ref, last_ref, len(tiles))


def run_experts(arrived, own_in, own_out, peer_in, peer_out):
    width, half_width = own_in.shape[1], own_out.shape[2]
    chunk = 256
    steps = half_width // chunk
    first = lambda h, s: jnp.where(h == 0, s, steps - 1)
    second = lambda h, s: jnp.where(h == 0, 0, s)
    block_in, block_out = (1, width, chunk), (1, width, chunk)
    specs = []
    for pick in (first, second):
        specs += [
            pl.BlockSpec(block_in, lambda h, s, pick=pick: (0, 0, pick(h, s))),
            pl.BlockSpec(block_in, lambda h, s, pick=pick: (0, 0, pick(h, s) + steps)),
            pl.BlockSpec(block_out, lambda h, s, pick=pick: (0, 0, pick(h, s))),
        ]
    rows = EXPERTS * CAP
    return pl.pallas_call(
        expert_kernel,
        grid=(2, steps),
        out_shape=jax.ShapeDtypeStruct(arrived.shape, arrived.dtype),
        in_specs=[pl.BlockSpec(memory_space=pltpu.VMEM)] + specs,
        out_specs=pl.BlockSpec(memory_space=pltpu.VMEM),
        scratch_shapes=[
            pltpu.VMEM((rows, width), jnp.bfloat16),
            pltpu.VMEM((rows, width), jnp.float32),
            pltpu.VMEM((EXPERTS * 24, 128), jnp.float32),
        ],
        compiler_params=pltpu.CompilerParams(vmem_limit_bytes=60 * 2**20),
        name="experts",
    )(arrived, own_in, own_in, own_out, peer_in, peer_in, peer_out)


def expert_layer(outgoing, hidden, routes, route_weights, own, peer):
    tokens_here, width = hidden.shape
    vmem = pl.BlockSpec(memory_space=pltpu.VMEM)
    arrived = exchange(outgoing, 1, "exchange_out")
    produced = run_experts(arrived, *own, *peer)
    returned = exchange(produced, 2, "exchange_back")
    mixed = pl.pallas_call(
        combine_kernel,
        out_shape=jax.ShapeDtypeStruct((width, tokens_here), jnp.bfloat16),
        in_specs=[vmem] * 4,
        out_specs=vmem,
        scratch_shapes=[pltpu.VMEM((EXPERTS * 24, 128), jnp.float32)],
        compiler_params=pltpu.CompilerParams(vmem_limit_bytes=40 * 2**20),
        name="combine",
    )(hidden, routes.T, route_weights.T, returned)
    return mixed.T


def shards(
    tokens,
    seg_ids,
    norm_gain,
    query_weight,
    kv_weight,
    out_weight,
    sinks,
    moe_gain,
    routes,
    route_weights,
    expert_in,
    expert_out,
):
    swap = [(c, c + 1 - 2 * (c % 2)) for c in range(lax.axis_size("col"))]
    own_in, own_out = expert_in, jnp.swapaxes(expert_out, 1, 2)
    peer_in, peer_out = (lax.ppermute(w, "col", swap) for w in (own_in, own_out))
    outgoing, hidden, kv_cache = attention_layer(
        tokens,
        seg_ids,
        norm_gain,
        query_weight,
        kv_weight,
        out_weight,
        sinks,
        moe_gain,
        routes,
    )
    mixed = expert_layer(
        outgoing, hidden, routes, route_weights, (own_in, own_out), (peer_in, peer_out)
    )
    return (mixed, kv_cache)


def solution(mesh):
    in_specs = (
        P(("col", "row"), None),
        P(("col", "row")),
        P(),
        P("col", "row"),
        P("col", "row"),
        P("row", "col"),
        P("row"),
        P(),
        P(("col", "row"), None),
        P(("col", "row"), None),
        P(("row", "col"), None, None),
        P(("row", "col"), None, None),
    )
    out_specs = (P(("col", "row"), None), P("col", "row"))
    return jax.shard_map(shards, mesh=mesh, in_specs=in_specs, out_specs=out_specs, check_vma=False)
```

time: 255 us -> 237 us (0.929)
  Pallas kernels: 238 us -> 225 us
  local copies, waits for them, and re-layouts: 13 us -> 5.35 us
    pallas_call x3 -> x1, Pallas kernels: 107 us -> 94.9 us  [attention_layer(): pl.pallas_call(functools.partial(front_kernel, width, share), out_shape=(...]
    unnamed x23 -> x11, local copies, waits for them, and re-layouts: 10.1 us -> 2.68 us
    reshape x4 -> x0, local copies, waits for them, and re-layouts: 2.86 us -> none  [the longest x1 1.23 us: attention_layer(): tokens.T.reshape(col_count, share, rows)]
  transfers between devices with their start and end apart: 2 -> 2, of which waited for: 0 -> 0; matrix products, arithmetic and copies ran while one was open for 2% -> 2% of each run, Pallas kernels for 63% -> 61%
where the time goes in v3:
time: 237 us; the launch traced here: 235 us
  Pallas kernels  225 us (95%)
  local copies, waits for them, and re-layouts  5.35 us (2%)
  other arithmetic  3.16 us (1%)
    pallas_call x2, Pallas kernels, exchange(): pl.pallas_call(exchange_kernel, out_shape=jax.ShapeDtypeStruct(messages.s...  101 us
    pallas_call x1, Pallas kernels, attention_layer(): pl.pallas_call(functools.partial(front_kernel, width, share), out_shape=(...  94.9 us
    pallas_call x1, Pallas kernels, run_experts(): pl.pallas_call(expert_kernel, grid=(2, steps), out_shape=jax.ShapeDtypeSt...  25.8 us
  transfers between devices with their start and end apart: 2, of which 0 were waited for; matrix products, arithmetic and copies ran while one was open for 2% of the time, Pallas kernels for 61%

profile of v3, /device:TPU:2, one launch (start us, length us, event | category | flops | bytes accessed | tf_op | source)
XLA Modules:
  0.0 235.2 jit_solution(9817924901106497819)
XLA Ops:
  0.6 0.1 collective-permute-start
  0.7 0.5 collective-permute-start.1
  1.2 0.7 stack.21
  1.9 0.7 stack.22
  2.6 0.7 fusion.9
  3.3 1.8 pad_maximum_fusion.shard_ref
  5.2 0.6 pad_maximum_fusion.1.gain_ref
  5.8 1.2 broadcast_in_dim.2.seg_ref
  7.1 94.9 %front.1 = (bf16[64,26,8,128]{3,2,1,0:T(8,128)(2,1)}, f32[128,2880]{1,0:T(8,128)}, bf16[1024,128]{1,0:T(8,128)(2,1)}) custom-call(bf16[2880,128]{1,0:T(8,128)(2,1)} %bitcast.18, f32[2,2880]{1,0:T(2,128)} %pad_maximum_fusion.1.gain_ref, s32[8,128]{1,0:T(8,128)} %broadcast_in_dim.2.seg_ref, f32[1,128]{1,0:T(1,128)} %constant.5.clone.freq_ref, ...), custom_call_target="tpu_custom_call" | custom-call | tf_op jit(solution)/shard_map/front/pallas_call | solution.py:613
  102.0 47.9 %exchange_out.1.in_ref = bf16[64,26,8,128]{3,2,1,0:T(8,128)(2,1)} custom-call(bf16[64,26,8,128]{3,2,1,0:T(8,128)(2,1)} %get-tuple-element.6.out_msgs), custom_call_target="tpu_custom_call" | custom-call | tf_op jit(solution)/shard_map/exchange_out/pallas_call | solution.py:86
  149.9 0.0 collective-permute-done.1.down_b
  149.9 0.0 collective-permute-done.gate_b.up_b
  149.9 25.8 %experts.1.out_msgs = bf16[64,26,8,128]{3,2,1,0:T(8,128)(2,1)} custom-call(bf16[64,26,8,128]{3,2,1,0:T(8,128)(2,1)} %exchange_out.1.in_ref, bf16[1,2880,1536]{2,1,0:T(8,128)(2,1)} %up_a.1, bf16[1,2880,1536]{2,1,0:T(8,128)(2,1)} %up_a.1, bf16[1,2880,768]{2,1,0:T(8,128)(2,1)} %bitcast.16, bf16[1,2880,1536]{2,1,0:T(8,128)(2,1)} %collective-permute-done.gate_b.up_b, ...), custom_call_target="tpu_custom_call" | custom-call | tf_op jit(solution)/shard_map/experts/pallas_call | solution.py:791
  175.7 0.0 copy-start.1
  175.7 0.0 copy-start.2
  175.8 0.0 copy-start.3
  175.8 0.0 copy-start.4
  175.8 53.3 %exchange_back.1.in_ref = bf16[64,26,8,128]{3,2,1,0:T(8,128)(2,1)} custom-call(bf16[64,26,8,128]{3,2,1,0:T(8,128)(2,1)} %experts.1.out_msgs), custom_call_target="tpu_custom_call" | custom-call | tf_op jit(solution)/shard_map/exchange_back/pallas_call | solution.py:86
  229.1 0.0 copy-done.1
  229.1 0.0 copy-done.2
  229.1 0.0 copy-done.3
  229.1 0.0 copy-start
  229.2 2.0 copy-done
  231.1 3.4 %combine.1 = bf16[2880,128]{1,0:T(8,128)(2,1)} custom-call(f32[128,2880]{1,0:T(8,128)S(1)} %copy-done.1, s32[4,128]{1,0:T(4,128)S(1)} %bitcast.13, f32[4,128]{1,0:T(4,128)S(1)} %bitcast.14, bf16[64,26,8,128]{3,2,1,0:T(8,128)(2,1)S(1)} %copy-done), custom_call_target="tpu_custom_call" | custom-call | tf_op jit(solution)/shard_map/combine/pallas_call | solution.py:813
  234.5 0.0 copy-done.4
  234.5 0.7 copy.16
  (1 shorter events, 0.0 us)
Async XLA Ops:
  0.6 149.3 %collective-permute-start = (bf16[1,2880,1536]{2,1,0:T(8,128)(2,1)}, bf16[1,2880,1536]{2,1,0:T(8,128)(2,1)}, u32[]{:S(2)}, u32[]{:S(2)}) collective-permute-start(bf16[1,2880,1536]{2,1,0:T(8,128)(2,1)} %up_a.1), channel_id=1, source_target_pairs={{0,1},{1,0},{2,3},{3,2},{4,5},{5,4},{6,7},{7,6},{8,9},{9,8},{10,11... | collective-permute-start | bytes 26542088 | tf_op jit(solution)/shard_map/ppermute | solution.py:841
  0.7 149.2 %collective-permute-start.1 = (bf16[1,2880,768]{2,1,0:T(8,128)(2,1)}, bf16[1,2880,768]{2,1,0:T(8,128)(2,1)}, u32[]{:S(2)}, u32[]{:S(2)}) collective-permute-start(bf16[1,2880,768]{2,1,0:T(8,128)(2,1)} %bitcast.15), channel_id=1, source_target_pairs={{0,1},{1,0},{2,3},{3,2},{4,5},{5,4},{6,7},{7,6},{8,9},{9,8},{10,11... | collective-permute-start | bytes 13271048 | tf_op jit(solution)/shard_map/ppermute | solution.py:841
  175.7 53.4 %copy-start.1 = (f32[128,2880]{1,0:T(8,128)S(1)}, f32[128,2880]{1,0:T(8,128)}, u32[]{:S(2)}) copy-start(f32[128,2880]{1,0:T(8,128)} %get-tuple-element.5.hidden_ref) | copy-start | bytes 4423684
  175.7 53.4 %copy-start.2 = (s32[128,4]{0,1:T(4,128)S(1)}, s32[128,4]{0,1:T(4,128)}, u32[]{:S(2)}) copy-start(s32[128,4]{0,1:T(4,128)} %param.21) | copy-start | bytes 6148
  175.8 53.4 %copy-start.3 = (f32[128,4]{0,1:T(4,128)S(1)}, f32[128,4]{0,1:T(4,128)}, u32[]{:S(2)}) copy-start(f32[128,4]{0,1:T(4,128)} %param.22) | copy-start | bytes 6148
  175.8 58.7 %copy-start.4 = (bf16[1024,128]{1,0:T(8,128)(2,1)S(1)}, bf16[1024,128]{1,0:T(8,128)(2,1)}, u32[]{:S(2)}) copy-start(bf16[1024,128]{1,0:T(8,128)(2,1)} %get-tuple-element.14) | copy-start | bytes 786436
  229.1 2.0 copy-start

commit v4 on v3

--- a/solution.py
+++ b/solution.py
@@ -45,57 +45,7 @@
     every = [
         (dx, (t + dx) % 4, (t // 4 + dx) % 4) for t in range(16) for dx in (1, 3, 2, 0)
     ]
-    return [v for v in every if v != (0, 0, 0)]
-
-
-def exchange_kernel(out_msgs, in_msgs, send_sem, recv_sem, own_sem):
-    x, y, z, core = chip_place()
-    me = expert_at(x, y, z)
-    offsets = hop_order()
-    barrier = pltpu.get_barrier_semaphore()
-    for dx, dy, dz in offsets:
-        pl.semaphore_signal(
-            barrier,
-            inc=1,
-            device_id=device_at((x + dx) % 4, (y + dy) % 4, (z + dz) % 4, core),
-            device_id_type=pl.DeviceIdType.MESH,
-        )
-    own = pltpu.make_async_copy(out_msgs.at[me], in_msgs.at[me], own_sem)
-    own.start()
-    pl.semaphore_wait(barrier, len(offsets))
-    copies = []
-    for number, (dx, dy, dz) in enumerate(offsets):
-        there = ((x + dx) % 4, (y + dy) % 4, (z + dz) % 4)
-        copy = pltpu.make_async_remote_copy(
-            src_ref=out_msgs.at[expert_at(*there)],
-            dst_ref=in_msgs.at[me],
-            send_sem=send_sem.at[number],
-            recv_sem=recv_sem.at[number],
-            device_id=device_at(*there, core),
-            device_id_type=pl.DeviceIdType.MESH,
-        )
-        copy.start()
-        copies.append(copy)
-    own.wait()
-    for copy in copies:
-        copy.wait()
-
-
-def exchange(messages, ident, name):
-    others = EXPERTS - 1
-    return pl.pallas_call(
-        exchange_kernel,
-        out_shape=jax.ShapeDtypeStruct(messages.shape, messages.dtype),
-        in_specs=[pl.BlockSpec(memory_space=pl.ANY)],
-        out_specs=pl.BlockSpec(memory_space=pl.ANY),
-        scratch_shapes=[
-            pltpu.SemaphoreType.DMA((others,)),
-            pltpu.SemaphoreType.DMA((others,)),
-            pltpu.SemaphoreType.DMA,
-        ],
-        compiler_params=pltpu.CompilerParams(collective_id=ident, has_side_effects=True),
-        name=name,
-    )(messages)
+    return [[v for v in every if sum(v) % 2 == odd] for odd in range(2)]
 
 
 def described(source, target, sems, number, device):
@@ -678,25 +628,27 @@
 
 
 def pack_message(out_ref, last_ref, tile_first, tile_last, k):
-    out_ref[:, k] = widen(tile_first).reshape(EXPERTS, 8, 128).astype(jnp.bfloat16)
-    last_ref[pl.ds(k, EXPERTS, stride=24), :] = widen(tile_last)
+    count = out_ref.shape[0]
+    out_ref[:, k] = widen(tile_first).reshape(count, 8, 128).astype(jnp.bfloat16)
+    last_ref[pl.ds(k, count, stride=24), :] = widen(tile_last)
 
 
 def finish_message(out_ref, last_ref, tile_count):
+    count = out_ref.shape[0]
     for k in range(tile_count, 24):
-        last_ref[pl.ds(k, EXPERTS, stride=24), :] = jnp.zeros((EXPERTS, 128), jnp.float32)
-    out_ref[:, tile_count:] = (
-        last_ref[...].reshape(EXPERTS, 3, 8, 128).astype(jnp.bfloat16)
-    )
+        last_ref[pl.ds(k, count, stride=24), :] = jnp.zeros((count, 128), jnp.float32)
+    out_ref[:, tile_count:] = last_ref[...].reshape(count, 3, 8, 128).astype(jnp.bfloat16)
 
 
 def unpack_last(in_ref, last_ref, tile_count):
-    last_ref[...] = in_ref[:, tile_count:].astype(jnp.float32).reshape(EXPERTS * 24, 128)
+    count = in_ref.shape[0]
+    last_ref[...] = in_ref[:, tile_count:].astype(jnp.float32).reshape(count * 24, 128)
 
 
 def unpack_tile(in_ref, last_ref, k):
-    first = in_ref[:, k].astype(jnp.float32).reshape(EXPERTS * 8, 128)
-    last = last_ref[pl.ds(k, EXPERTS, stride=24), :]
+    count = in_ref.shape[0]
+    first = in_ref[:, k].astype(jnp.float32).reshape(count * 8, 128)
+    last = last_ref[pl.ds(k, count, stride=24), :]
     return jnp.concatenate([first, last], axis=0).astype(jnp.bfloat16)
 
 
@@ -726,90 +678,163 @@
 
 
 def expert_kernel(
-    in_ref, gate_a, up_a, down_a, gate_b, up_b, down_b, out_ref, rows_ref, total_ref, last_ref
+    out_msgs,
+    own_in,
+    own_out,
+    peer_in,
+    peer_out,
+    back_msgs,
+    in_ref,
+    out_ref,
+    up_ref,
+    down_ref,
+    rows_ref,
+    total_ref,
+    last_ref,
+    send_sem,
+    recv_sem,
+    back_send_sem,
+    back_recv_sem,
+    own_sem,
 ):
-    half, step = pl.program_id(0), pl.program_id(1)
+    x, y, z, core = chip_place()
+    me = expert_at(x, y, z)
+    groups = hop_order()
+    order = groups[0] + groups[1]
+    in_group = len(groups[0])
     width = total_ref.shape[1]
     tiles = tiles_of(width)
-
-    @pl.when((half == 0) & (step == 0))
-    def _():
-        unpack_last(in_ref, last_ref, len(tiles))
+    chunk = 256
+    steps = down_ref.shape[2] // chunk
+
+    def there(offset, sign):
+        return tuple((here + sign * step + 4) % 4 for here, step in zip((x, y, z), offset))
+
+    loads = [
+        pltpu.make_async_copy(source.at[0], target, own_sem.at[n])
+        for n, (source, target) in enumerate(
+            (
+                (own_in, up_ref.at[0]),
+                (own_out, down_ref.at[0]),
+                (peer_in, up_ref.at[1]),
+                (peer_out, down_ref.at[1]),
+            )
+        )
+    ]
+    greet([device_at(*there(v, 1), core) for v in order if v != (0, 0, 0)])
+    arriving, going_back = [], []
+    for number, offset in enumerate(order):
+        if offset == (0, 0, 0):
+            copy = pltpu.make_async_copy(out_msgs.at[me], in_ref.at[number], own_sem.at[4])
+            copy.start()
+        else:
+            target = there(offset, 1)
+            copy = send(
+                out_msgs.at[expert_at(*target)],
+                in_ref.at[number],
+                (send_sem, recv_sem),
+                number,
+                device_at(*target, core),
+            )
+        arriving.append(copy)
+    for load in loads:
+        load.start()
+
+    for group in range(2):
+        first = group * in_group
+        here = pl.ds(first, in_group)
+        for number in range(first, first + in_group):
+            if order[number] == (0, 0, 0):
+                arriving[number].wait()
+            else:
+                arriving[number].wait_recv()
+        unpack_last(in_ref.at[here], last_ref, len(tiles))
         for k, start, wide in tiles:
-            rows_ref[:, start : start + wide] = unpack_tile(in_ref, last_ref, k)[:, :wide]
-
-    def run(gate, up, down, fresh):
-        rows = rows_ref[...]
-        gate_part = jnp.dot(rows, gate[0], preferred_element_type=jnp.float32)
-        up_part = jnp.dot(rows, up[0], preferred_element_type=jnp.float32)
-        act = (gate_part * jax.nn.sigmoid(glu_alpha * gate_part) * (up_part + 1.0)).astype(
-            jnp.bfloat16
-        )
-        part = lax.dot_general(
-            act, down[0], (((1,), (1,)), ((), ())), preferred_element_type=jnp.float32
-        )
-        if fresh:
-            total_ref[...] = part
-        else:
-            total_ref[...] += part
-
-    @pl.when((half == 0) & (step == 0))
-    def _():
-        run(gate_a, up_a, down_a, True)
-
-    @pl.when((half == 0) & (step != 0))
-    def _():
-        run(gate_a, up_a, down_a, False)
-
-    @pl.when(half == 1)
-    def _():
-        run(gate_b, up_b, down_b, False)
-
-    @pl.when((half == 1) & (step == pl.num_programs(1) - 1))
-    def _():
+            rows_ref[:, start : start + wide] = unpack_tile(in_ref.at[here], last_ref, k)[:, :wide]
+        if group == 0:
+            for load in loads:
+                load.wait()
+        total_ref[...] = jnp.zeros_like(total_ref)
+
+        def one_step(step, carry):
+            half, lane = step // steps, (step % steps) * chunk
+            gate_lanes = pl.ds(pl.multiple_of(lane, chunk), chunk)
+            up_lanes = pl.ds(pl.multiple_of(lane + steps * chunk, chunk), chunk)
+            rows = rows_ref[...]
+            gate_part = jnp.dot(
+                rows, up_ref[half, :, gate_lanes], preferred_element_type=jnp.float32
+            )
+            up_part = jnp.dot(rows, up_ref[half, :, up_lanes], preferred_element_type=jnp.float32)
+            act = (gate_part * jax.nn.sigmoid(glu_alpha * gate_part) * (up_part + 1.0)).astype(
+                jnp.bfloat16
+            )
+            total_ref[...] += lax.dot_general(
+                act,
+                down_ref[half, :, gate_lanes],
+                (((1,), (1,)), ((), ())),
+                preferred_element_type=jnp.float32,
+            )
+            return carry
+
+        lax.fori_loop(0, 2 * steps, one_step, 0)
         for k, start, wide in tiles:
             tile = total_ref[:, start : start + wide]
-            pack_message(out_ref, last_ref, tile[: EXPERTS * 8], tile[EXPERTS * 8 :], k)
-        finish_message(out_ref, last_ref, len(tiles))
-
-
-def run_experts(arrived, own_in, own_out, peer_in, peer_out):
-    width, half_width = own_in.shape[1], own_out.shape[2]
-    chunk = 256
-    steps = half_width // chunk
-    first = lambda h, s: jnp.where(h == 0, s, steps - 1)
-    second = lambda h, s: jnp.where(h == 0, 0, s)
-    block_in, block_out = (1, width, chunk), (1, width, chunk)
-    specs = []
-    for pick in (first, second):
-        specs += [
-            pl.BlockSpec(block_in, lambda h, s, pick=pick: (0, 0, pick(h, s))),
-            pl.BlockSpec(block_in, lambda h, s, pick=pick: (0, 0, pick(h, s) + steps)),
-            pl.BlockSpec(block_out, lambda h, s, pick=pick: (0, 0, pick(h, s))),
-        ]
-    rows = EXPERTS * CAP
+            pack_message(
+                out_ref.at[here], last_ref, tile[: in_group * 8], tile[in_group * 8 :], k
+            )
+        finish_message(out_ref.at[here], last_ref, len(tiles))
+        for number in range(first, first + in_group):
+            if order[number] == (0, 0, 0):
+                copy = pltpu.make_async_copy(out_ref.at[number], back_msgs.at[me], own_sem.at[5])
+                copy.start()
+            else:
+                copy = send(
+                    out_ref.at[number],
+                    back_msgs.at[me],
+                    (back_send_sem, back_recv_sem),
+                    number,
+                    device_at(*there(order[number], -1), core),
+                )
+            going_back.append(copy)
+    for number, copy in enumerate(arriving):
+        if order[number] != (0, 0, 0):
+            copy.wait_send()
+    for copy in going_back:
+        copy.wait()
+
+
+def run_experts(outgoing, own_in, own_out, peer_in, peer_out):
+    width, hidden_width = own_in.shape[1:]
+    hbm = pl.BlockSpec(memory_space=pl.ANY)
+    rows = EXPERTS * CAP // 2
+    sem = pltpu.SemaphoreType.DMA
     return pl.pallas_call(
         expert_kernel,
-        grid=(2, steps),
-        out_shape=jax.ShapeDtypeStruct(arrived.shape, arrived.dtype),
-        in_specs=[pl.BlockSpec(memory_space=pltpu.VMEM)] + specs,
-        out_specs=pl.BlockSpec(memory_space=pltpu.VMEM),
+        out_shape=jax.ShapeDtypeStruct(outgoing.shape, outgoing.dtype),
+        in_specs=[hbm] * 5,
+        out_specs=hbm,
         scratch_shapes=[
+            pltpu.VMEM(outgoing.shape, jnp.bfloat16),
+            pltpu.VMEM(outgoing.shape, jnp.bfloat16),
+            pltpu.VMEM((2, width, hidden_width), jnp.bfloat16),
+            pltpu.VMEM((2, width, hidden_width // 2), jnp.bfloat16),
             pltpu.VMEM((rows, width), jnp.bfloat16),
             pltpu.VMEM((rows, width), jnp.float32),
-            pltpu.VMEM((EXPERTS * 24, 128), jnp.float32),
-        ],
-        compiler_params=pltpu.CompilerParams(vmem_limit_bytes=60 * 2**20),
+            pltpu.VMEM((EXPERTS // 2 * 24, 128), jnp.float32),
+        ]
+        + [sem((EXPERTS,))] * 4
+        + [sem((6,))],
+        compiler_params=pltpu.CompilerParams(
+            collective_id=1, has_side_effects=True, vmem_limit_bytes=60 * 2**20
+        ),
         name="experts",
-    )(arrived, own_in, own_in, own_out, peer_in, peer_in, peer_out)
+    )(outgoing, own_in, own_out, peer_in, peer_out)
 
 
 def expert_layer(outgoing, hidden, routes, route_weights, own, peer):
     tokens_here, width = hidden.shape
     vmem = pl.BlockSpec(memory_space=pltpu.VMEM)
-    arrived = exchange(outgoing, 1, "exchange_out")
-    produced = run_experts(arrived, *own, *peer)
-    returned = exchange(produced, 2, "exchange_back")
+    returned = run_experts(outgoing, *own, *peer)
     mixed = pl.pallas_call(
         combine_kernel,
         out_shape=jax.ShapeDtypeStruct((width, tokens_here), jnp.bfloat16),

time: 237 us -> 213 us (0.90)
  Pallas kernels: 225 us -> 197 us
    pallas_call x3 -> x1, Pallas kernels: 127 us -> 98.8 us  [run_experts(): pl.pallas_call(expert_kernel, out_shape=jax.ShapeDtypeStruct(outgoing.sha...]
    unnamed x11 -> x13, local copies, waits for them, and re-layouts: 2.68 us -> 4.78 us
  transfers between devices with their start and end apart: 2 -> 2, of which waited for: 0 -> 0; matrix products, arithmetic and copies ran while one was open for 2% -> 3% of each run, Pallas kernels for 61% -> 45%
where the time goes in v4:
time: 213 us; the launch traced here: 209 us
  Pallas kernels  197 us (92%)
  local copies, waits for them, and re-layouts  7.46 us (4%)
  other arithmetic  3.16 us (1%)
    pallas_call x1, Pallas kernels, run_experts(): pl.pallas_call(expert_kernel, out_shape=jax.ShapeDtypeStruct(outgoing.sha...  98.8 us
    pallas_call x1, Pallas kernels, attention_layer(): pl.pallas_call(functools.partial(front_kernel, width, share), out_shape=(...  94.9 us
    unnamed x13, local copies, waits for them, and re-layouts  4.78 us
  transfers between devices with their start and end apart: 2, of which 0 were waited for; matrix products, arithmetic and copies ran while one was open for 3% of the time, Pallas kernels for 45%

profile of v4, /device:TPU:2, one launch (start us, length us, event | category | flops | bytes accessed | tf_op | source)
XLA Modules:
  0.0 209.0 jit_solution(428633657820874984)
XLA Ops:
  0.6 0.1 collective-permute-start
  0.7 0.5 collective-permute-start.1
  1.2 0.7 stack.21
  1.9 0.7 stack.22
  2.6 0.7 fusion.9
  3.3 1.8 pad_maximum_fusion.shard_ref
  5.2 0.6 pad_maximum_fusion.1.gain_ref
  5.8 1.2 broadcast_in_dim.2.seg_ref
  7.1 94.9 %front.1 = (bf16[64,26,8,128]{3,2,1,0:T(8,128)(2,1)}, f32[128,2880]{1,0:T(8,128)}, bf16[1024,128]{1,0:T(8,128)(2,1)}) custom-call(bf16[2880,128]{1,0:T(8,128)(2,1)} %bitcast.18, f32[2,2880]{1,0:T(2,128)} %pad_maximum_fusion.1.gain_ref, s32[8,128]{1,0:T(8,128)} %broadcast_in_dim.2.seg_ref, f32[1,128]{1,0:T(1,128)} %constant.5.clone.freq_ref, ...), custom_call_target="tpu_custom_call" | custom-call | tf_op jit(solution)/shard_map/front/pallas_call | solution.py:563
  102.0 0.0 collective-permute-done.1.peer_out
  102.0 0.0 copy-start.4
  102.0 0.0 collective-permute-done.peer_in
  102.0 2.1 %copy-done.4 = bf16[1,2880,768]{2,1,0:T(8,128)(2,1)} copy-done((bf16[1,2880,768]{2,1,0:T(8,128)(2,1)}, bf16[1,2880,768]{2,1,0:T(8,128)(2,1)S(1)}, u32[]{:S(2)}) %copy-start.4) | copy-done | bytes 4423704
  104.1 0.0 copy-start.1
  104.1 0.0 copy-start.2
  104.1 0.0 copy-start.3
  104.1 0.0 copy-start.5
  104.1 98.8 %experts.1.in_ref = bf16[64,26,8,128]{3,2,1,0:T(8,128)(2,1)} custom-call(bf16[64,26,8,128]{3,2,1,0:T(8,128)(2,1)} %get-tuple-element.6.out_msgs, bf16[1,2880,1536]{2,1,0:T(8,128)(2,1)} %own_in.1, bf16[1,2880,768]{2,1,0:T(8,128)(2,1)} %bitcast.16, bf16[1,2880,1536]{2,1,0:T(8,128)(2,1)} %collective-permute-done.peer_in, bf16[1,2880,768]{2,1,0:T(8,128)(2,1)} %copy-done.4), custom_call_target="tpu_custom_call" | custom-call | tf_op jit(solution)/shard_map/experts/pallas_call | solution.py:811
  202.9 0.0 copy-done.1
  202.9 0.0 copy-done.2
  202.9 0.0 copy-done.3
  203.0 0.0 copy-start
  203.0 2.0 copy-done
  204.9 3.4 %combine.1 = bf16[2880,128]{1,0:T(8,128)(2,1)} custom-call(f32[128,2880]{1,0:T(8,128)S(1)} %copy-done.1, s32[4,128]{1,0:T(4,128)S(1)} %bitcast.13, f32[4,128]{1,0:T(4,128)S(1)} %bitcast.14, bf16[64,26,8,128]{3,2,1,0:T(8,128)(2,1)S(1)} %copy-done), custom_call_target="tpu_custom_call" | custom-call | tf_op jit(solution)/shard_map/combine/pallas_call | solution.py:838
  208.3 0.0 copy-done.5
  208.3 0.7 copy.16
  (1 shorter events, 0.0 us)
Async XLA Ops:
  0.6 101.4 %collective-permute-start = (bf16[1,2880,1536]{2,1,0:T(8,128)(2,1)}, bf16[1,2880,1536]{2,1,0:T(8,128)(2,1)}, u32[]{:S(2)}, u32[]{:S(2)}) collective-permute-start(bf16[1,2880,1536]{2,1,0:T(8,128)(2,1)} %own_in.1), channel_id=1, source_target_pairs={{0,1},{1,0},{2,3},{3,2},{4,5},{5,4},{6,7},{7,6},{8,9},{9,8},{10,11... | collective-permute-start | bytes 26542088 | tf_op jit(solution)/shard_map/ppermute | solution.py:866
  0.7 101.3 %collective-permute-start.1 = (bf16[1,2880,768]{2,1,0:T(8,128)(2,1)}, bf16[1,2880,768]{2,1,0:T(8,128)(2,1)S(1)}, u32[]{:S(2)}, u32[]{:S(2)}) collective-permute-start(bf16[1,2880,768]{2,1,0:T(8,128)(2,1)} %bitcast.15), channel_id=1, source_target_pairs={{0,1},{1,0},{2,3},{3,2},{4,5},{5,4},{6,7},{7,6},{8,9},{9,8},{10,11... | collective-permute-start | bytes 13271048 | tf_op jit(solution)/shard_map/ppermute | solution.py:866
  102.0 2.1 %copy-start.4 = (bf16[1,2880,768]{2,1,0:T(8,128)(2,1)}, bf16[1,2880,768]{2,1,0:T(8,128)(2,1)S(1)}, u32[]{:S(2)}) copy-start(bf16[1,2880,768]{2,1,0:T(8,128)(2,1)S(1)} %collective-permute-done.1.peer_out) | copy-start | bytes 13271044
  104.1 98.8 %copy-start.1 = (f32[128,2880]{1,0:T(8,128)S(1)}, f32[128,2880]{1,0:T(8,128)}, u32[]{:S(2)}) copy-start(f32[128,2880]{1,0:T(8,128)} %get-tuple-element.5.hidden_ref) | copy-start | bytes 4423684
  104.1 98.8 %copy-start.2 = (s32[128,4]{0,1:T(4,128)S(1)}, s32[128,4]{0,1:T(4,128)}, u32[]{:S(2)}) copy-start(s32[128,4]{0,1:T(4,128)} %param.21) | copy-start | bytes 6148
  104.1 98.8 %copy-start.3 = (f32[128,4]{0,1:T(4,128)S(1)}, f32[128,4]{0,1:T(4,128)}, u32[]{:S(2)}) copy-start(f32[128,4]{0,1:T(4,128)} %param.22) | copy-start | bytes 6148
  104.1 104.2 %copy-start.5 = (bf16[1024,128]{1,0:T(8,128)(2,1)S(1)}, bf16[1024,128]{1,0:T(8,128)(2,1)}, u32[]{:S(2)}) copy-start(bf16[1024,128]{1,0:T(8,128)(2,1)} %get-tuple-element.14) | copy-start | bytes 786436
  203.0 2.0 copy-start
